TPU v7x, 256 devices: a whole 4x4x8 slice. The times are simulated.
256 devices in a mesh: section: 4 (over x), seq: 16 (over z, y_lo), dp: 4 (over y_hi, core).
Axes of the slice: x: 4, y: 4 (y_hi: 2, y_lo: 2; y = y_hi * 2 + y_lo), z: 8, core: 2. Of those that a mesh axis runs over, the one named last changes fastest.
Arguments:
- main_hidden: bfloat16 [4, 4, 2048, 7168], P('section', 'dp', 'seq'), may hold values from -6 to 6
- embedded: bfloat16 [4, 4, 2048, 7168], P('section', 'dp', 'seq'), may hold values from -6 to 6
- cotangent: bfloat16 [4, 4, 2048, 7168], P('section', 'dp', 'seq'), may hold values from -6 to 6
- slot_token: int32 [4, 4, 2, 96], P('section', 'dp', None, 'seq'), may hold values from 0 to 127, as said below
- slot_count: int32 [4, 4, 2, 16], P('section', 'dp', None, 'seq'), may hold values from 1 to 6, as said below
- route_gate: float32 [4, 4, 2, 96], P('section', 'dp', None, 'seq'), may hold values from 0.2 to 2
- norm_gain: float32 [2, 2, 7168], replicated, may hold values from 0.5 to 1.5
- expert_weight: bfloat16 [2, 3, 7168, 2048], P(None, None, 'seq', 'dp'), may hold values from -0.0625 to 0.0625
Outputs:
- hidden_grad: bfloat16 [4, 4, 2048, 7168], P('section', 'dp', 'seq')
- expert_grad: bfloat16 [4, 2, 3, 7168, 2048], P('section', None, None, 'seq', 'dp')
- gain_grad: float32 [4, 2, 2, 7168], P('section', None, None, ('seq', 'dp'))
Inputs may be any that keep to these rules, and one draw needn't show every extreme that they name: `slot_token`: the slots of one device and depth name distinct positions of that device's block. `slot_count`: in every micro-batch, sequence and depth some device has all 6 slots live.
All inputs are finite; a program needn't handle non-finite values.
Results may differ from a plain program's by a relative error of at most 0.0077.
Values may be sent and summed in bfloat16 or wider, within the bound.
A program may use at most 128 MiB of HBM per device.

v0:
```python
import jax
import jax.numpy as jnp
from jax import lax
from jax.sharding import PartitionSpec as P

eps_norm = 1e-06


def from_behind(value, axis, steps):
    count = lax.axis_size(axis)
    pairs = [(source, (source + steps) % count) for source in range(count)]
    return lax.ppermute(value, axis, pairs)


def from_behind_2(array, axis, by):
    size = lax.axis_size(axis)
    pairs = [(i, i + by) for i in range(size) if 0 <= i + by < size]
    return lax.ppermute(array, axis, pairs)


def normed(value):
    wide = value.astype(jnp.float32)
    scale = lax.rsqrt(jnp.mean(wide * wide, axis=-1, keepdims=True) + eps_norm)
    return (wide * scale, scale)


def norm_back(grad, unit, scale):
    inner = jnp.mean(grad * unit, axis=-1, keepdims=True)
    return (grad - unit * inner) * scale


def contract_rows(left, right):
    return lax.dot_general(
        left, right, (((0,), (0,)), ((), ())), preferred_element_type=jnp.float32
    )


def contract_last(left, right):
    return lax.dot_general(
        left, right, (((1,), (1,)), ((), ())), preferred_element_type=jnp.float32
    )


def spread_rows(rows):
    parts = lax.all_to_all(rows, "seq", split_axis=1, concat_axis=0, tiled=True)
    return lax.all_gather(parts, "dp", axis=0, tiled=True)


def return_rows(partial_rows, capacity):
    blocks = partial_rows.reshape(
        lax.axis_size("dp"), lax.axis_size("seq"), capacity, partial_rows.shape[1]
    )
    back = lax.all_to_all(blocks, "seq", split_axis=1, concat_axis=3, tiled=True)
    total = lax.psum_scatter(back, "dp", scatter_dimension=0, tiled=True)
    return total.reshape(capacity, -1)


def pre_grads(d_act, gate_in, up_in):
    sig = jax.nn.sigmoid(gate_in)
    d_gate = (d_act * up_in * sig * (1.0 + gate_in * (1.0 - sig))).astype(jnp.bfloat16)
    d_up = (d_act * jax.nn.silu(gate_in)).astype(jnp.bfloat16)
    return (d_gate, d_up)


def local(
    main_hidden, embedded, cotangent, slot_token, slot_count, route_gate, norm_gain, expert_weight
):
    depths = norm_gain.shape[0]
    tokens_here = main_hidden.shape[2]
    capacity = slot_token.shape[3]
    hidden = from_behind(main_hidden, "section", 1)[0, 0]
    own_rows = embedded[0, 0]
    ahead = from_behind_2(own_rows[:depths], "seq", -1)
    padded = jnp.concatenate([own_rows, ahead], 0)
    places = jnp.arange(capacity, dtype=jnp.int32)
    current = hidden
    saved = []
    for depth in range(depths):
        shifted = padded[depth + 1 : depth + 1 + tokens_here]
        unit_h, scale_h = normed(current)
        unit_e, scale_e = normed(shifted)
        mixed = (unit_h * norm_gain[depth, 0] + unit_e * norm_gain[depth, 1]).astype(jnp.bfloat16)
        tokens = slot_token[0, 0, depth]
        live = places < slot_count[0, 0, depth, 0]
        weight = route_gate[0, 0, depth] * live.astype(jnp.float32)
        rows = mixed[tokens] * live[:, None].astype(jnp.bfloat16)
        quarter = spread_rows(rows)
        gate_part = jnp.dot(quarter, expert_weight[depth, 0], preferred_element_type=jnp.float32)
        up_part = jnp.dot(quarter, expert_weight[depth, 1], preferred_element_type=jnp.float32)
        gate_in, up_in = lax.psum((gate_part, up_part), "seq")
        act = (jax.nn.silu(gate_in) * up_in).astype(jnp.bfloat16)
        result = return_rows(contract_last(act, expert_weight[depth, 2]), capacity)
        current = (
            mixed.astype(jnp.float32).at[tokens].add(result * weight[:, None]).astype(jnp.bfloat16)
        )
        saved.append((unit_h, scale_h, unit_e, tokens, live, weight, quarter, gate_in, up_in, act))
    grad = cotangent[0, 0].astype(jnp.float32)
    weight_grads = [None] * depths
    gain_terms = [None] * depths
    for depth in reversed(range(depths)):
        unit_h, scale_h, unit_e, tokens, live, weight, quarter, gate_in, up_in, act = saved[depth]
        dout = (grad[tokens] * weight[:, None]).astype(jnp.bfloat16)
        dout_quarter = spread_rows(dout)
        act_part = jnp.dot(
            dout_quarter, expert_weight[depth, 2], preferred_element_type=jnp.float32
        )
        down_grad = contract_rows(dout_quarter, act)
        d_act = lax.psum(act_part, "seq")
        d_gate, d_up = pre_grads(d_act, gate_in, up_in)
        gate_grad = contract_rows(quarter, d_gate)
        up_grad = contract_rows(quarter, d_up)
        partial_rows = contract_last(d_gate, expert_weight[depth, 0]) + contract_last(
            d_up, expert_weight[depth, 1]
        )
        d_rows = return_rows(partial_rows, capacity)
        d_mixed = grad.at[tokens].add(d_rows * live[:, None].astype(jnp.float32))
        gain_terms[depth] = jnp.stack([jnp.sum(d_mixed * unit_h, 0), jnp.sum(d_mixed * unit_e, 0)])
        weight_grads[depth] = jnp.stack([gate_grad, up_grad, down_grad])
        grad = norm_back(d_mixed * norm_gain[depth, 0], unit_h, scale_h)
    gain_grad = lax.psum_scatter(
        jnp.stack(gain_terms), ("seq", "dp"), scatter_dimension=2, tiled=True
    )
    hidden_grad = from_behind(grad.astype(jnp.bfloat16)[None, None], "section", -1)
    expert_grad = jnp.stack(weight_grads).astype(jnp.bfloat16)[None]
    return (hidden_grad, expert_grad, gain_grad[None])


def solution(mesh):
    return jax.shard_map(
        local,
        mesh=mesh,
        in_specs=(
            P("section", "dp", "seq", None),
            P("section", "dp", "seq", None),
            P("section", "dp", "seq", None),
            P("section", "dp", None, "seq"),
            P("section", "dp", None, "seq"),
            P("section", "dp", None, "seq"),
            P(),
            P(None, None, "seq", "dp"),
        ),
        out_specs=(
            P("section", "dp", "seq", None),
            P("section", None, None, "seq", "dp"),
            P("section", None, None, ("seq", "dp")),
        ),
        check_vma=False,
    )
```

profile of v0, /device:TPU:1, one launch (start us, length us, event | category | flops | bytes accessed | tf_op | source)
XLA Modules:
  0.0 1102.2 jit_solution(5909491801143368804)
XLA Ops:
  15.3 3.7 fusion.18
  19.0 31.6 %collective-permute-done = bf16[1,1,128,7168]{3,2,1,0:T(8,128)(2,1)S(1)} collective-permute-done((bf16[1,1,128,7168]{3,2,1,0:T(8,128)(2,1)}, bf16[1,1,128,7168]{3,2,1,0:T(8,128)(2,1)S(1)}, u32[]{:S(2)}, u32[]{:S(2)}) %collective-permute-start) | collective-permute-done | bytes 1835040 | tf_op jit(solution)/shard_map/ppermute | solution.py:12
  51.0 3.4 fusion.87
  54.5 2.4 gather_fusion.1
  57.2 20.3 %all_to_all.118 = bf16[6,16,448]{2,0,1:T(8,128)(2,1)S(1)} all-to-all(bf16[6,16,448]{2,0,1:T(8,128)(2,1)S(1)} %copy.77), channel_id=1, replica_groups=mesh['section'=4,'seq'=16,'dp'=4] {'seq'}, dimensions={1} | all-to-all | bytes 172032 | tf_op jit(solution)/shard_map/all_to_all | solution.py:45
  77.5 11.1 %all_gather.13 = bf16[384,448]{1,0:T(8,128)(2,1)S(1)} all-gather(bf16[96,448]{1,0:T(8,128)(2,1)S(1)} %all_to_all.92), channel_id=1, replica_groups=mesh['section'=4,'seq'=16,'dp'=4] {'dp'}, dimensions={0}, use_global_device_ids=true | all-gather | bytes 430080 | tf_op jit(solution)/shard_map/all_gather | solution.py:46
  93.3 127.7 %all-reduce.10.cloned.1.call-done = (f32[384,512]{1,0:T(8,128)}, f32[384,512]{1,0:T(8,128)}) async-done(((f32[384,512]{1,0:T(8,128)}, f32[384,512]{1,0:T(8,128)}), (f32[384,512]{1,0:T(8,128)}, f32[384,512]{1,0:T(8,128)})) %all-reduce.10.cloned.1.call-update) | async-done | bytes 1572880 | tf_op jit(solution)/shard_map/psum | solution.py:90
  224.7 19.5 %all_to_all.119 = f32[4,16,6,448]{3,0,2,1:T(4,128)S(1)} all-to-all(f32[4,16,6,448]{3,0,2,1:T(4,128)S(1)} %copy.79), channel_id=1, replica_groups=mesh['section'=4,'seq'=16,'dp'=4] {'seq'}, dimensions={1} | all-to-all | bytes 1376256 | tf_op jit(solution)/shard_map/all_to_all | solution.py:53
  245.9 3.7 bitcast_convert_fusion
  249.6 2.7 gather_fusion
  254.5 3.5 all-to-all-start
  258.7 7.9 all-to-all-done
  266.7 23.7 %all_gather.12 = bf16[384,448]{1,0:T(8,128)(2,1)S(1)} all-gather(bf16[96,448]{1,0:T(8,128)(2,1)S(1)} %all_to_all.89), channel_id=1, replica_groups=mesh['section'=4,'seq'=16,'dp'=4] {'dp'}, dimensions={0}, use_global_device_ids=true | all-gather | bytes 430080 | tf_op jit(solution)/shard_map/all_gather | solution.py:46
  292.6 5.1 scatter_custom_fusion
  297.7 2.6 fusion.23
  301.6 2.5 fusion.13
  304.0 2.4 gather_fusion.2
  307.4 4.5 all-to-all-start.3
  314.4 6.0 all-to-all-done.3
  320.5 9.8 all_gather.14
  334.8 135.8 %all-reduce.8.cloned.1.call-done = (f32[384,512]{1,0:T(8,128)}, f32[384,512]{1,0:T(8,128)}, f32[384,512]{1,0:T(8,128)}) async-done(((f32[384,512]{1,0:T(8,128)}, f32[384,512]{1,0:T(8,128)}, f32[384,512]{1,0:T(8,128)}), (f32[384,512]{1,0:T(8,128)}, f32[384,512]{1,0:T(8,128)}, f32[384,512]{1,0:T(8,128)})) %all-reduce.8.cloned.1.call-update) | async-done | bytes 2359312 | tf_op jit(solution)/shard_map/psum | solution.py:90
  474.3 2.3 convolution_add_fusion.1
  476.6 2.3 copy.83
  482.9 19.9 %all_to_all.120 = f32[4,16,6,448]{3,0,2,1:T(4,128)S(1)} all-to-all(f32[4,16,6,448]{3,0,2,1:T(4,128)S(1)} %copy.84), channel_id=1, replica_groups=mesh['section'=4,'seq'=16,'dp'=4] {'seq'}, dimensions={1} | all-to-all | bytes 1376256 | tf_op jit(solution)/shard_map/all_to_all | solution.py:53
  504.2 2.4 reshape.296
  507.3 41.6 %reduce-scatter.9.cloned.1.call-done = f32[1,1,6,7168]{3,2,1,0:T(8,128)} async-done(((f32[4,1,6,7168]{3,2,1,0:T(8,128)}), f32[1,1,6,7168]{3,2,1,0:T(8,128)}) %reduce-scatter.9.cloned.1.call-update) | async-done | bytes 172048 | tf_op jit(solution)/shard_map/reduce_scatter | solution.py:54
  549.0 5.1 scatter_custom_fusion.1
  554.0 4.9 fusion.22
  559.0 2.6 fusion.21
  561.6 2.8 gather_fusion.3
  564.7 15.1 %all_to_all.121 = bf16[6,16,448]{2,0,1:T(8,128)(2,1)S(1)} all-to-all(bf16[6,16,448]{2,0,1:T(8,128)(2,1)S(1)} %copy.87), channel_id=1, replica_groups=mesh['section'=4,'seq'=16,'dp'=4] {'seq'}, dimensions={1} | all-to-all | bytes 172032 | tf_op jit(solution)/shard_map/all_to_all | solution.py:45
  579.9 9.7 all_gather.15
  592.7 123.0 %all-reduce.6.cloned.1.call-done = f32[384,512]{1,0:T(8,128)} async-done(((f32[384,512]{1,0:T(8,128)}), f32[384,512]{1,0:T(8,128)}) %all-reduce.6.cloned.1.call-update) | async-done | bytes 786448 | tf_op jit(solution)/shard_map/psum | solution.py:108
  726.1 2.6 copy.89
  728.8 5.2 all-to-all-start.6
  738.1 2.8 fusion.38
  740.9 7.8 all-to-all-done.6
  748.7 2.5 copy.95
  751.2 2.4 reshape.297
  753.9 2.6 maximum_bitcast_fusion.1
  759.5 40.1 %reduce-scatter.11.cloned.1.call-done = f32[1,1,6,7168]{3,2,1,0:T(8,128)} async-done(((f32[4,1,6,7168]{3,2,1,0:T(8,128)}), f32[1,1,6,7168]{3,2,1,0:T(8,128)}) %reduce-scatter.11.cloned.1.call-update) | async-done | bytes 172048 | tf_op jit(solution)/shard_map/reduce_scatter | solution.py:54
  799.6 5.1 scatter_custom_fusion.2
  804.7 4.3 fusion.29
  811.2 2.4 collective-permute-start.2
  813.7 6.8 copy.96
  820.6 7.9 reshape.298
  831.9 259.1 %reduce-scatter.13.cloned.1.call-done = f32[112,4]{1,0:T(8,128)} async-done(((f32[7168,4]{1,0:T(8,128)}), f32[112,4]{1,0:T(8,128)}) %reduce-scatter.13.cloned.1.call-update) | async-done | bytes 1808
  1092.5 2.8 copy.113
  (141 shorter events, 71.4 us)
Async XLA Ops:
  7.2 213.8 %all-reduce.10.cloned.1.call-start = ((), (), s32[]{:S(2)}) async-start(), calls=%async_computation.17 | async-start | bytes 3145728 | tf_op jit(solution)/shard_map/psum | solution.py:90
  8.1 7.2 collective-permute-start.1
  9.4 41.1 %collective-permute-start = (bf16[1,1,128,7168]{3,2,1,0:T(8,128)(2,1)}, bf16[1,1,128,7168]{3,2,1,0:T(8,128)(2,1)S(1)}, u32[]{:S(2)}, u32[]{:S(2)}) collective-permute-start(bf16[1,1,128,7168]{3,2,1,0:T(8,128)(2,1)} %param.8), channel_id=1, source_target_pairs={{0,64},{64,128},{128,192},{192,0},{1,65},{65,129},{129,193},{193,1... | collective-permute-start | bytes 5505032 | tf_op jit(solution)/shard_map/ppermute | solution.py:12
  12.3 280.3 %copy-start.25 = (s32[6]{0:T(128)}, s32[6]{0:T(128)S(1)}, u32[]{:S(2)}) copy-start(s32[6]{0:T(128)S(1)} %get-tuple-element.32) | copy-start | bytes 76
  13.6 40.8 %copy-start.18 = (s32[1024]{0:T(1024)}, s32[1024]{0:T(1024)S(1)}, u32[]{:S(2)}) copy-start(s32[1024]{0:T(1024)S(1)} %pad_clamp_fusion) | copy-start | bytes 12292
  19.0 35.5 %copy-start.5 = (bf16[128,7168]{1,0:T(8,128)(2,1)}, bf16[128,7168]{1,0:T(8,128)(2,1)S(1)}, u32[]{:S(2)}) copy-start(bf16[128,7168]{1,0:T(8,128)(2,1)S(1)} %get-tuple-element.19) | copy-start | bytes 5505028
  19.0 35.5 %copy-start.23 = (f32[128]{0:T(128)}, f32[128]{0:T(128)S(1)}, u32[]{:S(2)}) copy-start(f32[128]{0:T(128)S(1)} %add_rsqrt_fusion.2) | copy-start | bytes 1540
  51.0 3.5 copy-start.19
  93.2 199.4 %reduce-scatter.7.cloned.1.call-start = ((), (), s32[]{:S(2)}) async-start(), calls=%async_computation.11 | async-start | bytes 1146880 | tf_op jit(solution)/shard_map/reduce_scatter | solution.py:54
  222.6 23.3 %copy-start.7 = (bf16[384,512]{1,0:T(8,128)(2,1)}, bf16[384,512]{1,0:T(8,128)(2,1)S(1)}, u32[]{:S(2)}) copy-start(bf16[384,512]{1,0:T(8,128)(2,1)S(1)} %multiply_convert_fusion.5) | copy-start | bytes 1179652
  245.9 6.5 copy-start.26
  253.7 46.6 %copy-start.21 = (f32[6]{0:T(128)}, f32[6]{0:T(128)S(1)}, u32[]{:S(2)}) copy-start(f32[6]{0:T(128)S(1)} %get-tuple-element.30) | copy-start | bytes 76
  254.5 12.1 %all-to-all-start = ((bf16[6,16,448]{2,0,1:T(8,128)(2,1)}), bf16[6,16,448]{2,0,1:T(8,128)(2,1)S(1)}, u32[]{:S(2)}, u32[]{:S(2)}) async-start(bf16[6,16,448]{2,0,1:T(8,128)(2,1)} %copy.76), calls=%async_computation | async-start | bytes 262144 | tf_op jit(solution)/shard_map/all_to_all | solution.py:45
  290.4 21.8 %copy-start.16 = (bf16[384,448]{1,0:T(8,128)(2,1)}, bf16[384,448]{1,0:T(8,128)(2,1)S(1)}, u32[]{:S(2)}) copy-start(bf16[384,448]{1,0:T(8,128)(2,1)S(1)} %all_gather.12) | copy-start | bytes 1032196
  297.7 3.9 copy-start.4
  300.3 1.2 copy-start.2
  307.4 13.0 %all-to-all-start.3 = ((bf16[6,16,448]{2,0,1:T(8,128)(2,1)}), bf16[6,16,448]{2,0,1:T(8,128)(2,1)S(1)}, u32[]{:S(2)}, u32[]{:S(2)}) async-start(bf16[6,16,448]{2,0,1:T(8,128)(2,1)} %copy.82), calls=%async_computation.4 | async-start | bytes 262144 | tf_op jit(solution)/shard_map/all_to_all | solution.py:45
  311.9 158.7 %all-reduce.8.cloned.1.call-start = ((), (), s32[]{:S(2)}) async-start(), calls=%async_computation.16 | async-start | bytes 4718592 | tf_op jit(solution)/shard_map/psum | solution.py:90
  334.8 214.2 %reduce-scatter.9.cloned.1.call-start = ((), (), s32[]{:S(2)}) async-start(), calls=%async_computation.12 | async-start | bytes 1146880 | tf_op jit(solution)/shard_map/reduce_scatter | solution.py:54
  472.7 1.6 copy-start.9
  506.6 209.1 %all-reduce.6.cloned.1.call-start = ((), (), s32[]{:S(2)}) async-start(), calls=%async_computation.13 | async-start | bytes 1572864 | tf_op jit(solution)/shard_map/psum | solution.py:108
  554.0 4.9 copy-start.1
  554.0 5.0 copy-start.3
  559.0 5.6 copy-start.22
  589.6 0.7 copy-start.10
  717.8 1.6 copy-start.12
  728.8 19.9 %all-to-all-start.6 = ((f32[4,16,6,448]{3,0,2,1:T(4,128)}), f32[4,16,6,448]{3,0,2,1:T(4,128)}, u32[]{:S(2)}, u32[]{:S(2)}) async-start(f32[4,16,6,448]{3,0,2,1:T(4,128)} %copy.89), calls=%async_computation.8 | async-start | bytes 1572864 | tf_op jit(solution)/shard_map/all_to_all | solution.py:53
  734.0 65.6 %reduce-scatter.11.cloned.1.call-start = ((), (), s32[]{:S(2)}) async-start(), calls=%async_computation.14 | async-start | bytes 1146880 | tf_op jit(solution)/shard_map/reduce_scatter | solution.py:54
  740.9 15.6 %copy-start.17 = (f32[7168]{0:T(1024)S(1)}, f32[7168]{0:T(1024)}, u32[]{:S(2)}) copy-start(f32[7168]{0:T(1024)} %get-tuple-element.8) | copy-start | bytes 86020
  740.9 15.7 %copy-start.8 = (bf16[384,512]{1,0:T(8,128)(2,1)S(1)}, bf16[384,512]{1,0:T(8,128)(2,1)}, u32[]{:S(2)}) copy-start(bf16[384,512]{1,0:T(8,128)(2,1)} %copy-done.7) | copy-start | bytes 1179652
  740.9 15.7 %copy-start.11 = (bf16[384,448]{1,0:T(8,128)(2,1)S(1)}, bf16[384,448]{1,0:T(8,128)(2,1)}, u32[]{:S(2)}) copy-start(bf16[384,448]{1,0:T(8,128)(2,1)} %copy-done.10) | copy-start | bytes 1032196
  753.6 337.3 %reduce-scatter.13.cloned.1.call-start = ((), (), s32[]{:S(2)}) async-start(), calls=%async_computation.15 | async-start | bytes 3727360
  753.9 3.9 copy-start.13
  756.6 48.1 %copy-start.20 = (f32[128]{0:T(128)S(1)}, f32[128]{0:T(128)}, u32[]{:S(2)}) copy-start(f32[128]{0:T(128)} %copy-done.19) | copy-start | bytes 1540
  756.6 48.1 %copy-start.24 = (f32[128]{0:T(128)S(1)}, f32[128]{0:T(128)}, u32[]{:S(2)}) copy-start(f32[128]{0:T(128)} %copy-done.23) | copy-start | bytes 1540
  804.7 4.4 copy-start
  811.2 281.4 %collective-permute-start.2 = (bf16[1,1,128,7168]{3,2,1,0:T(8,128)(2,1)}, bf16[1,1,128,7168]{3,2,1,0:T(8,128)(2,1)}, u32[]{:S(2)}, u32[]{:S(2)}) collective-permute-start(bf16[1,1,128,7168]{3,2,1,0:T(8,128)(2,1)} %fusion.32), channel_id=1, source_target_pairs={{0,192},{64,0},{128,64},{192,128},{1,193},{65,1},{129,65},{193,129... | collective-permute-start | bytes 5505032 | tf_op jit(solution)/shard_map/ppermute | solution.py:12
  828.5 1.0 copy-start.14
  828.5 1.2 copy-start.15
  828.5 1.6 copy-start.6
Sparse Core Ops, SparseCore 0:
  93.3 127.5 all-reduce.9
  246.0 46.5 reduce-scatter.6
  334.9 135.6 all-reduce.7
  506.8 42.1 reduce-scatter.8
  592.8 122.8 all-reduce.5
  753.8 45.7 reduce-scatter.10
  828.6 262.2 reduce-scatter.12
where the time goes:
time: 1110 us; the launch traced here: 1100 us
  waiting for transfers between devices  783 us (71%)
  blocking collectives  129 us (12%)
  local copies, waits for them, and re-layouts  63.1 us (6%)
  other arithmetic  60.9 us (5%)
  matrix products  31.8 us (3%)
  starting transfers between devices  19.8 us (2%)
  between operations  14.6 us (1%)
    psum x2, waiting for transfers between devices, local(): gate_in, up_in = lax.psum((gate_part, up_part), 'seq')  263 us
    unnamed x8, waiting for transfers between devices  259 us
    psum x1, waiting for transfers between devices, local(): d_act = lax.psum(act_part, 'seq')  123 us
    reduce_scatter x3, waiting for transfers between devices, return_rows(): total = lax.psum_scatter(back, 'dp', scatter_dimension=0, tiled=True)  84 us
    all_gather x4, blocking collectives, spread_rows(): return lax.all_gather(parts, 'dp', axis=0, tiled=True)  54.3 us
    all_to_all x2, blocking collectives, return_rows(): lax.all_to_all(blocks, 'seq', split_axis=1, concat_axis=3, tiled=True)  39.4 us
    all_to_all x2, blocking collectives, spread_rows(): parts = lax.all_to_all(rows, 'seq', split_axis=1, concat_axis=0, tiled=True)  35.4 us
    ppermute x2, waiting for transfers between devices, from_behind(): return lax.ppermute(value, axis, pairs)  31.6 us
  transfers between devices with their start and end apart: 13, of which 11 were waited for; matrix products, arithmetic and copies ran while one was open for 5% of the time, Pallas kernels for 0%

commit v1 on v0

v1 whole, which is shorter than its diff:
```python
import functools

import jax
import jax.numpy as jnp
from jax import lax
from jax.experimental import pallas as pl
from jax.experimental.pallas import tpu as pltpu
from jax.sharding import PartitionSpec as P

eps_norm = 1e-06
MESH = pl.DeviceIdType.MESH
F32 = jnp.float32
BF16 = jnp.bfloat16
PK = 16


def from_behind(value, axis, steps):
    count = lax.axis_size(axis)
    pairs = [(source, (source + steps) % count) for source in range(count)]
    return lax.ppermute(value, axis, pairs)


def from_ahead(array, axis, by):
    size = lax.axis_size(axis)
    pairs = [(i, i - by) for i in range(size) if 0 <= i - by < size]
    return lax.ppermute(array, axis, pairs)


def normed(value):
    wide = value.astype(F32)
    scale = lax.rsqrt(jnp.mean(wide * wide, axis=-1, keepdims=True) + eps_norm)
    return (wide * scale, scale)


def norm_back(grad, unit, scale):
    inner = jnp.mean(grad * unit, axis=-1, keepdims=True)
    return (grad - unit * inner) * scale


def dot_nn(a, b):
    return lax.dot_general(a, b, (((1,), (0,)), ((), ())), preferred_element_type=F32)


def dot_nt(a, b):
    return lax.dot_general(a, b, (((1,), (1,)), ((), ())), preferred_element_type=F32)


def dot_tn(a, b):
    return lax.dot_general(a, b, (((0,), (0,)), ((), ())), preferred_element_type=F32)


class Wires:
    def __init__(self, send, recv):
        self.send, self.recv = send, recv
        self.phases = 0
        self.open = []

    def copy(self, src, dst, ph, slot_s, slot_r, axis, to):
        return pltpu.make_async_remote_copy(
            src_ref=src,
            dst_ref=dst,
            send_sem=self.send.at[ph, slot_s],
            recv_sem=self.recv.at[ph, slot_r],
            device_id={axis: to},
            device_id_type=MESH,
        )

    def start(self, axis, size, me, src_of, dst):
        ph = self.phases
        self.phases += 1

        def body(o, c):
            to = lax.rem(me + o, size)
            self.copy(src_of(to), dst, ph, o, me, axis, to).start()
            return c

        lax.fori_loop(1, size, body, 0)
        self.open.append((ph, axis, size, me, src_of))
        return ph

    def wait(self, ph, axis, size, me, dst_of):
        def body(o, c):
            frm = lax.rem(me + o, size)
            self.copy(dst_of(frm), dst_of(frm), ph, o, frm, axis, frm).wait_recv()
            return c

        lax.fori_loop(1, size, body, 0)

    def drain(self):
        for ph, axis, size, me, src_of in self.open:

            def body(o, c):
                to = lax.rem(me + o, size)
                self.copy(src_of(to), src_of(to), ph, o, me, axis, to).wait_send()
                return c

            lax.fori_loop(1, size, body, 0)


def greet(axes):
    barrier = pltpu.get_barrier_semaphore()
    total = 0
    for axis, size, me in axes:

        def body(o, c):
            to = lax.rem(me + o, size)
            pl.semaphore_signal(barrier, inc=1, device_id={axis: to}, device_id_type=MESH)
            return c

        lax.fori_loop(1, size, body, 0)
        total += size - 1
    pl.semaphore_wait(barrier, total)


def chain_kernel(S, Q, C, D, pk, meta, g2, w, eg, ret, land, mland, rows, xr, do, gu, lg, da, ld,
                 act, dg, op, lo, pv, ss, ssl, od, rb, gsv, send, recv):
    me = lax.axis_index("seq")
    d = lax.axis_index("dp")
    DS, HS = w.shape[2], w.shape[3]
    RW = C * S
    CG = S // Q
    PC = HS // CG
    rg, cg = me // CG, lax.rem(me, CG)
    wires = Wires(send, recv)

    def rowslice(g):
        return pl.ds(pl.multiple_of(g * RW, 32 if RW % 32 == 0 else 8), RW)

    def piece_of(ref):
        def src(to):
            return ref.at[to % CG, :, rowslice(to // CG), :]
        return src

    def seq_start(src_of, dst):
        return wires.start("seq", S, me, src_of, dst)

    def seq_wait(ph, dst_of):
        wires.wait(ph, "seq", S, me, dst_of)

    def dp_start(src_of, dst):
        return wires.start("dp", Q, d, src_of, dst)

    def dp_wait(ph, dst_of):
        wires.wait(ph, "dp", Q, d, dst_of)

    greet((("seq", S, me), ("dp", Q, d)))

    def blk(b):
        return pl.ds(pl.multiple_of(b * PK, PK), PK)

    ph_b = seq_start(lambda to: pk.at[0, to], land.at[0, blk(me), :])
    ph_m = seq_start(lambda to: meta, mland.at[me])
    ph_a = seq_start(lambda to: pk.at[1, to], land.at[1, blk(me), :])
    land[0, blk(me), :] = pk[0, me]
    land[1, blk(me), :] = pk[1, me]
    mland[me] = meta[...]

    def unpack(k):
        r = lax.broadcasted_iota(jnp.int32, (S * PK, S * PK), 0)
        c = lax.broadcasted_iota(jnp.int32, (S * PK, S * PK), 1)
        perm = jnp.where(c == (r % S) * PK + r // S, 1.0, 0.0).astype(BF16)
        rows[k] = dot_nn(perm, land[k])

    def rows_at(k, slot):
        return rows[k, slot * S:(slot + 1) * S, :]

    def gather_dp(k, dst):
        return dp_start(lambda to: dst.at[k, rowslice(d), :], dst.at[k, rowslice(d), :])

    def gather_dp_wait(ph, k, dst):
        dp_wait(ph, lambda frm: dst.at[k, rowslice(frm), :])

    def gate_up(k):
        for half in range(2):
            full = dot_nn(xr[k], w[k, half]).astype(BF16)
            for q in range(CG):
                gu[k, q, half] = full[:, q * PC:(q + 1) * PC]
        ph = seq_start(piece_of(gu.at[k]), lg.at[k, me])
        lg[k, me] = gu[k, cg, :, rowslice(rg), :]
        return ph

    def gate_up_wait(ph, k):
        seq_wait(ph, lambda frm: lg.at[k, frm])
        return add_up(lg.at[k])

    def add_up(ref):
        total = ref[0].astype(F32)
        for b in range(1, ref.shape[0]):
            total = total + ref[b].astype(F32)
        return total

    def dact(k):
        full = dot_nn(do[k], w[k, 2]).astype(BF16)
        for q in range(CG):
            da[k, q, 0] = full[:, q * PC:(q + 1) * PC]
        ph = seq_start(piece_of(da.at[k]), ld.at[k, me])
        ld[k, me] = da[k, cg, :, rowslice(rg), :]
        return ph

    def dact_wait(ph, k):
        seq_wait(ph, lambda frm: ld.at[k, frm])
        return add_up(ld.at[k])[0]

    def spread_piece(ref):
        mine = ref.at[cg, :, rowslice(rg), :]
        return seq_start(lambda to: mine, mine)

    def spread_wait(ph, ref):
        seq_wait(ph, lambda frm: ref.at[lax.rem(frm, CG), :, rowslice(frm // CG), :])

    def reduce_dp(n, full):
        op[n] = full.astype(BF16)
        ph = dp_start(lambda to: op.at[n, rowslice(to), :], lo.at[n, d])
        lo[n, d] = op[n, rowslice(d), :]
        return ph

    def reduce_dp_wait(ph, n):
        dp_wait(ph, lambda frm: lo.at[n, frm])
        return add_up(lo.at[n])

    def drows(k):
        total = None
        for q in range(CG):
            cols = slice(q * PC, (q + 1) * PC)
            part = dot_nt(dg[k, q, 0], w[k, 0, :, cols]) + dot_nt(dg[k, q, 1], w[k, 1, :, cols])
            total = part if total is None else total + part
        return total

    def sums_start(n, cols):
        lane = lax.broadcasted_iota(jnp.int32, (S, 128), 1)
        total = jnp.zeros((S, 128), F32)
        for i, col in enumerate(cols):
            total = total + jnp.where(lane == i, col, 0.0)
        ss[n] = total
        ph = seq_start(lambda to: ss.at[n], ssl.at[n, me])
        ssl[n, me] = total
        return ph

    def sums_wait(ph, n):
        seq_wait(ph, lambda frm: ssl.at[n, frm])
        return add_up(ssl.at[n]) * (1.0 / D)

    def pre_grads(k, d_act):
        gate, up = gsv[k, 0], gsv[k, 1]
        sig = 1.0 / (1.0 + jnp.exp(-gate))
        dg[k, cg, 0, rowslice(rg), :] = (d_act * up * sig * (1.0 + gate * (1.0 - sig))).astype(BF16)
        dg[k, cg, 1, rowslice(rg), :] = (d_act * (gate * sig)).astype(BF16)

    def act_piece(k):
        gate, up = gsv[k, 0], gsv[k, 1]
        act[k, cg, 0, rowslice(rg), :] = (gate / (1.0 + jnp.exp(-gate)) * up).astype(BF16)

    def in_grads(k):
        for half in range(2):
            for q in range(CG):
                eg[k, half, :, q * PC:(q + 1) * PC] = dot_tn(xr[k], dg[k, q, half]).astype(BF16)

    def down_grad(k):
        for q in range(CG):
            eg[k, 2, :, q * PC:(q + 1) * PC] = dot_tn(do[k], act[k, q, 0]).astype(BF16)

    seq_wait(ph_b, lambda frm: land.at[0, blk(frm), :])
    unpack(0)
    xr[0, rowslice(d), :] = rows[0, 0:RW, :].astype(BF16)
    ph_x = gather_dp(0, xr)
    seq_wait(ph_a, lambda frm: land.at[1, blk(frm), :])
    unpack(1)
    do[1, rowslice(d), :] = rows[1, C * S:2 * C * S, :].astype(BF16)
    ph_d2 = gather_dp(1, do)
    gather_dp_wait(ph_x, 0, xr)
    ph = gate_up(0)
    gather_dp_wait(ph_d2, 1, do)
    gsv[0] = gate_up_wait(ph, 0)
    act_piece(0)
    ph = spread_piece(act.at[0])
    spread_wait(ph, act.at[0])
    out = None
    for q in range(CG):
        part = dot_nt(act[0, q, 0], w[0, 2, :, q * PC:(q + 1) * PC])
        out = part if out is None else out + part
    ph = reduce_dp(0, out)
    ph_da2 = dact(1)
    seq_wait(ph_m, lambda frm: mland.at[frm])
    facts = jnp.sum(mland[...], axis=1)

    def fact(k):
        return facts[:, k:k + 1]

    def ov(j, i):
        return fact(16 + j * C + i)

    out = reduce_dp_wait(ph, 0)
    od[0:RW, :] = out.astype(BF16)
    cols = []
    for i in range(C):
        before = rows_at(0, i) + fact(i) * out[i * S:(i + 1) * S]
        before = before.astype(BF16).astype(F32)
        pv[i * S:(i + 1) * S, :] = before
        cols.append(jnp.sum(before * before, axis=1, keepdims=True))
    for j in range(C):
        before = rows_at(0, C + j)
        for i in range(C):
            before = before + (ov(j, i) * fact(i)) * out[i * S:(i + 1) * S]
        before = before.astype(BF16).astype(F32)
        pv[(C + j) * S:(C + j + 1) * S, :] = before
        cols.append(jnp.sum(before * before, axis=1, keepdims=True))
    ph = sums_start(0, cols)
    gain_h, gain_e = g2[0:1, :], g2[1:2, :]
    scale = lax.rsqrt(sums_wait(ph, 0) + eps_norm)

    for j in range(C):
        unit = pv[(C + j) * S:(C + j + 1) * S, :] * scale[:, C + j:C + j + 1]
        mixed = unit * gain_h + (rows_at(1, j) * fact(8 + j)) * gain_e
        od[RW + j * S:RW + (j + 1) * S, :] = mixed.astype(BF16)
    xr[1, rowslice(d), :] = od[RW:2 * RW, :]
    ph = gather_dp(1, xr)
    gather_dp_wait(ph, 1, xr)
    ph = gate_up(1)
    d_act = dact_wait(ph_da2, 1)
    gsv[1] = gate_up_wait(ph, 1)
    pre_grads(1, d_act)
    ph = spread_piece(dg.at[1])
    act_piece(1)
    ph_a2 = spread_piece(act.at[1])
    spread_wait(ph, dg.at[1])
    ph = reduce_dp(1, drows(1))
    in_grads(1)
    back = reduce_dp_wait(ph, 1)
    od[RW:2 * RW, :] = back.astype(BF16)
    cols, keep_u, keep_n = [], [], []
    for i in range(C):
        cot = rows_at(1, 2 * C + i) if i < PK - 2 * C else rows_at(0, 2 * C + i - (PK - 2 * C))
        for j in range(C):
            cot = cot + ov(j, i) * back[j * S:(j + 1) * S]
        u = cot * gain_h
        unit = pv[i * S:(i + 1) * S, :] * scale[:, i:i + 1]
        keep_u.append(u)
        keep_n.append(unit)
        cols.append(jnp.sum(u * unit, axis=1, keepdims=True))
    ph = sums_start(1, cols)

    def send_back(k, lo_row, hi_row):
        r = lax.broadcasted_iota(jnp.int32, (S * PK, hi_row - lo_row), 0)
        c = lax.broadcasted_iota(jnp.int32, (S * PK, hi_row - lo_row), 1)
        perm = jnp.where(c == (r % PK) * S + r // PK, 1.0, 0.0).astype(BF16)
        rb[k] = dot_nn(perm, od[lo_row:hi_row, :]).astype(BF16)
        ph = seq_start(lambda to: rb.at[k, blk(to), :], ret.at[k, me])
        ret[k, me] = rb[k, blk(me), :]
        return ph

    inner = sums_wait(ph, 1)

    for i in range(C):
        back = (keep_u[i] - keep_n[i] * inner[:, i:i + 1]) * scale[:, i:i + 1]
        rows[1, i * S:(i + 1) * S, :] = back * fact(i)
    do[0, rowslice(d), :] = rows[1, 0:RW, :].astype(BF16)
    ph = gather_dp(0, do)
    gather_dp_wait(ph, 0, do)
    ph = dact(0)
    spread_wait(ph_a2, act.at[1])
    down_grad(1)
    down_grad(0)
    d_act = dact_wait(ph, 0)
    pre_grads(0, d_act)
    ph = spread_piece(dg.at[0])
    ph_r0 = send_back(0, 0, 2 * RW)
    spread_wait(ph, dg.at[0])
    ph = reduce_dp(2, drows(0))
    in_grads(0)
    back = reduce_dp_wait(ph, 2)
    od[2 * RW:3 * RW, :] = back.astype(BF16)
    ph_r1 = send_back(1, 2 * RW, 3 * RW)
    seq_wait(ph_r0, lambda frm: ret.at[0, frm])
    seq_wait(ph_r1, lambda frm: ret.at[1, frm])
    wires.drain()


def chain(pk, meta, g2, w, C, D):
    S, Q = lax.axis_size("seq"), lax.axis_size("dp")
    DS, HS = w.shape[2], w.shape[3]
    RW = C * S
    NR = Q * RW
    CG = S // Q
    PC = HS // CG
    vm = pltpu.VMEM
    phases = 24
    return pl.pallas_call(
        functools.partial(chain_kernel, S, Q, C, D),
        out_shape=(
            jax.ShapeDtypeStruct(w.shape, BF16),
            jax.ShapeDtypeStruct((2, S, PK, DS), BF16),
        ),
        in_specs=[pl.BlockSpec(memory_space=vm)] * 4,
        out_specs=(pl.BlockSpec(memory_space=vm),) * 2,
        scratch_shapes=[
            vm((2, S * PK, DS), BF16),
            vm((S, 8, 128), F32),
            vm((2, S * PK, DS), F32),
            vm((2, NR, DS), BF16),
            vm((2, NR, DS), BF16),
            vm((2, CG, 2, NR, PC), BF16),
            vm((2, S, 2, RW, PC), BF16),
            vm((2, CG, 1, NR, PC), BF16),
            vm((2, S, 1, RW, PC), BF16),
            vm((2, CG, 1, NR, PC), BF16),
            vm((2, CG, 2, NR, PC), BF16),
            vm((3, NR, DS), BF16),
            vm((3, Q, RW, DS), BF16),
            vm((2 * RW, DS), F32),
            vm((2, S, 128), F32),
            vm((2, S, S, 128), F32),
            vm((3 * RW, DS), BF16),
            vm((2, S * PK, DS), BF16),
            vm((2, 2, RW, PC), F32),
            pltpu.SemaphoreType.DMA((phases, S)),
            pltpu.SemaphoreType.DMA((phases, S)),
        ],
        compiler_params=pltpu.CompilerParams(
            collective_id=0, has_side_effects=True, vmem_limit_bytes=56 * 1024 * 1024
        ),
        cost_estimate=pl.CostEstimate(flops=4 * 10**9, bytes_accessed=150 * 10**6, transcendentals=10**6),
        name="expert_chain",
    )(pk, meta, g2, w)


def gain_kernel(S, Q, parts, total, land, mine, land2, send, recv):
    me = lax.axis_index("seq")
    d = lax.axis_index("dp")
    wires = Wires(send, recv)
    greet((("seq", S, me), ("dp", Q, d)))
    ph = wires.start("seq", S, me, lambda to: parts.at[to], land.at[me])
    land[me] = parts[me]
    wires.wait(ph, "seq", S, me, lambda frm: land.at[frm])
    value = land[0]
    for b in range(1, S):
        value = value + land[b]
    mine[...] = value
    ph = wires.start("dp", Q, d, lambda to: mine, land2.at[d])
    land2[d] = value
    wires.wait(ph, "dp", Q, d, lambda frm: land2.at[frm])
    value = land2[0]
    for b in range(1, Q):
        value = value + land2[b]
    total[...] = value
    wires.drain()


def gain_sum(parts):
    S, Q = lax.axis_size("seq"), lax.axis_size("dp")
    shape = parts.shape[1:]
    vm = pltpu.VMEM
    return pl.pallas_call(
        functools.partial(gain_kernel, S, Q),
        out_shape=jax.ShapeDtypeStruct(shape, F32),
        in_specs=[pl.BlockSpec(memory_space=vm)],
        out_specs=pl.BlockSpec(memory_space=vm),
        scratch_shapes=[
            vm((S,) + shape, F32),
            vm(shape, F32),
            vm((Q,) + shape, F32),
            pltpu.SemaphoreType.DMA((2, S)),
            pltpu.SemaphoreType.DMA((2, S)),
        ],
        compiler_params=pltpu.CompilerParams(collective_id=1, has_side_effects=True),
        cost_estimate=pl.CostEstimate(flops=10**6, bytes_accessed=30 * 10**6, transcendentals=0),
        name="gain_sum",
    )(parts)


def pick(index, count):
    return (index[:, None] == jnp.arange(count, dtype=jnp.int32)[None, :]).astype(BF16)


def put_rows(tokens, rows, weight, count):
    at = (jnp.arange(count, dtype=jnp.int32)[:, None] == tokens[None, :]).astype(F32)
    at = at * weight[None, :]
    total = None
    for i in range(rows.shape[0]):
        part = at[:, i:i + 1] * rows[i:i + 1]
        total = part if total is None else total + part
    return total


def local(main_hidden, embedded, cotangent, slot_token, slot_count, route_gate, norm_gain, w):
    S = lax.axis_size("seq")
    me = lax.axis_index("seq")
    tokens_here, D = main_hidden.shape[2:]
    C = slot_token.shape[3]
    DS = D // S
    tok = slot_token[0, 0]
    live = (jnp.arange(C, dtype=jnp.int32)[None, :] < slot_count[0, 0]).astype(F32)
    weight = route_gate[0, 0] * live
    own, cot = embedded[0, 0], cotangent[0, 0]
    ahead = from_ahead(own[:2], "seq", 1)

    asked = from_behind(tok, "section", -1).reshape(-1)
    sent = dot_nn(pick(asked, tokens_here), main_hidden[0, 0]).astype(BF16)
    h_rows = from_behind(sent, "section", 1)
    bulk, h_rows = lax.optimization_barrier((main_hidden, h_rows))
    hidden = from_behind(bulk, "section", 1)[0, 0]

    flat = tok.reshape(-1)
    places = jnp.concatenate([flat + 1, tok[1] + 2])
    e_pick = pick(places, tokens_here + 2)
    e_rows = dot_nn(e_pick[:, :tokens_here], own) + dot_nn(e_pick[:, tokens_here:], ahead)
    c_rows = dot_nn(pick(flat, tokens_here), cot)
    unit_h, _ = normed(h_rows)
    unit_e, _ = normed(e_rows[:2 * C])
    mixed = (unit_h * norm_gain[0, 0] + unit_e * norm_gain[0, 1]).astype(BF16)
    e2 = e_rows[2 * C:]
    _, se2 = normed(e2)
    m1 = mixed[:C] * live[0][:, None].astype(BF16)
    e2 = (e2 * live[1][:, None]).astype(BF16)
    dout2 = (c_rows[C:] * weight[1][:, None]).astype(BF16)
    c1 = c_rows[:C].astype(BF16)
    cut = PK - 2 * C
    pad = jnp.zeros((2 * PK - 5 * C, D), BF16)
    pk_b = jnp.concatenate([m1, mixed[C:], c1[cut:], pad], 0)
    pk_a = jnp.concatenate([e2, dout2, c1[:cut]], 0)
    pk = jnp.stack([pk_b, pk_a]).reshape(2, PK, S, DS).transpose(0, 2, 1, 3)
    same = (tok[1][:, None] == tok[0][None, :]).astype(F32) * live[1][:, None] * live[0][None, :]
    facts = jnp.concatenate(
        [weight[0], jnp.zeros((8 - C,), F32), se2[:, 0], jnp.zeros((8 - C,), F32), same.reshape(-1)]
    )
    meta = jnp.zeros((8, 128), F32).at[0, :facts.shape[0]].set(facts)
    g2 = lax.dynamic_slice(norm_gain[1], (0, me * DS), (2, DS))
    g2 = jnp.concatenate([g2, jnp.zeros((6, DS), F32)], 0)

    expert_grad, ret = chain(pk, meta, g2, w, C, D)
    ret = ret.transpose(0, 2, 1, 3).reshape(2, PK, D).astype(F32)
    out1, back2, back1 = ret[0, :C], ret[0, C:2 * C], ret[1, :C]

    padded = jnp.concatenate([own, ahead], 0)
    unit_h1, scale_h1 = normed(hidden)
    unit_e1, _ = normed(padded[1:1 + tokens_here])
    unit_e2, _ = normed(padded[2:2 + tokens_here])
    mixed1 = (unit_h1 * norm_gain[0, 0] + unit_e1 * norm_gain[0, 1]).astype(BF16)
    prev2 = (mixed1.astype(F32) + put_rows(tok[0], out1, weight[0], tokens_here)).astype(BF16)
    unit_h2, scale_h2 = normed(prev2)
    dm2 = cot.astype(F32) + put_rows(tok[1], back2, live[1], tokens_here)
    g2h, g2e = jnp.sum(dm2 * unit_h2, 0), jnp.sum(dm2 * unit_e2, 0)
    grad1 = norm_back(dm2 * norm_gain[1, 0], unit_h2, scale_h2)
    dm1 = grad1 + put_rows(tok[0], back1, live[0], tokens_here)
    g1h, g1e = jnp.sum(dm1 * unit_h1, 0), jnp.sum(dm1 * unit_e1, 0)
    grad0 = norm_back(dm1 * norm_gain[0, 0], unit_h1, scale_h1)
    hidden_grad = from_behind(grad0.astype(BF16)[None, None], "section", -1)

    parts = jnp.stack([g1h, g1e, g2h, g2e]).reshape(4, S, DS).transpose(1, 0, 2)
    parts = jnp.concatenate([parts, jnp.zeros((S, 4, DS), F32)], 1)
    total = gain_sum(parts)
    Q = lax.axis_size("dp")
    wide = DS // Q
    gain_grad = lax.dynamic_slice(total, (0, lax.axis_index("dp") * wide), (4, wide))
    return (hidden_grad, expert_grad[None], gain_grad.reshape(1, 2, 2, wide))


def solution(mesh):
    return jax.shard_map(
        local,
        mesh=mesh,
        in_specs=(
            P("section", "dp", "seq", None),
            P("section", "dp", "seq", None),
            P("section", "dp", "seq", None),
            P("section", "dp", None, "seq"),
            P("section", "dp", None, "seq"),
            P("section", "dp", None, "seq"),
            P(),
            P(None, None, "seq", "dp"),
        ),
        out_specs=(
            P("section", "dp", "seq", None),
            P("section", None, None, "seq", "dp"),
            P("section", None, None, ("seq", "dp")),
        ),
        check_vma=False,
    )
```

time: 1110 us -> 319 us (0.29)
  waiting for transfers between devices: 783 us -> 16.1 us
  Pallas kernels: 0 us -> 230 us
  blocking collectives: 129 us -> 0 us
  local copies, waits for them, and re-layouts: 63.1 us -> 24.4 us
  other arithmetic: 60.9 us -> 29.8 us
  matrix products: 31.8 us -> 6.58 us
  between operations: 14.6 us -> 1.26 us
  starting transfers between devices: 19.8 us -> 8.25 us
    psum x3 -> x0, waiting for transfers between devices: 387 us -> none  [the longest x2 263 us: local(): gate_in, up_in = lax.psum((gate_part, up_part), 'seq')]
    unnamed x8 -> x0, waiting for transfers between devices: 259 us -> none
    pallas_call x0 -> x2, Pallas kernels: none -> 230 us  [the longest x1 209 us: chain(): pl.pallas_call(functools.partial(chain_kernel, S, Q, C, D), out_shape=(ja...]
    reduce_scatter x3 -> x0, waiting for transfers between devices: 84 us -> none  [return_rows(): total = lax.psum_scatter(back, 'dp', scatter_dimension=0, tiled=True)]
    all_to_all x4 -> x0, blocking collectives: 74.8 us -> none  [the longest x2 39.4 us: return_rows(): lax.all_to_all(blocks, 'seq', split_axis=1, concat_axis=3, tiled=True)]
    all_gather x4 -> x0, blocking collectives: 54.3 us -> none  [spread_rows(): return lax.all_gather(parts, 'dp', axis=0, tiled=True)]
    dot_general x17 -> x4, matrix products: 31.8 us -> 6.58 us  [dot_nn(): lax.dot_general(a, b, (((1,), (0,)), ((), ())), preferred_element_type=F32)]
    all_to_all x3 -> x0, waiting for transfers between devices: 21.7 us -> none  [the longest x2 13.9 us: spread_rows(): parts = lax.all_to_all(rows, 'seq', split_axis=1, concat_axis=0, tiled=True)]
  transfers between devices with their start and end apart: 13 -> 5, of which waited for: 11 -> 1; matrix products, arithmetic and copies ran while one was open for 5% -> 11% of each run, Pallas kernels for 0% -> 73%
where the time goes in v1:
time: 319 us; the launch traced here: 316 us
  Pallas kernels  230 us (72%)
  other arithmetic  29.8 us (9%)
  local copies, waits for them, and re-layouts  24.4 us (8%)
  waiting for transfers between devices  16.1 us (5%)
  starting transfers between devices  8.25 us (3%)
  matrix products  6.58 us (2%)
    pallas_call x1, Pallas kernels, chain(): pl.pallas_call(functools.partial(chain_kernel, S, Q, C, D), out_shape=(ja...  209 us
    pallas_call x1, Pallas kernels, gain_sum(): pl.pallas_call(functools.partial(gain_kernel, S, Q), out_shape=jax.ShapeD...  21.2 us
    ppermute x4, waiting for transfers between devices, from_behind(): return lax.ppermute(value, axis, pairs)  16.1 us
    reduce_sum x6, other arithmetic, normed(): scale = lax.rsqrt(jnp.mean(wide * wide, axis=-1, keepdims=True) + eps_norm)  8.92 us
    ppermute x4, starting transfers between devices, from_behind(): return lax.ppermute(value, axis, pairs)  6.95 us
    dot_general x4, matrix products, dot_nn(): lax.dot_general(a, b, (((1,), (0,)), ((), ())), preferred_element_type=F32)  6.58 us
    reduce_sum x1, other arithmetic, local(): g1h, g1e = (jnp.sum(dm1 * unit_h1, 0), jnp.sum(dm1 * unit_e1, 0))  6.55 us
  transfers between devices with their start and end apart: 5, of which 1 were waited for; matrix products, arithmetic and copies ran while one was open for 11% of the time, Pallas kernels for 73%

profile of v1, /device:TPU:1, one launch (start us, length us, event | category | flops | bytes accessed | tf_op | source)
XLA Modules:
  0.0 316.4 jit_solution(15669521858126961634)
XLA Ops:
  0.7 3.4 %collective-permute-start = (s32[2,6]{1,0:T(2,128)}, s32[2,6]{1,0:T(2,128)S(1)}, u32[]{:S(2)}, u32[]{:S(2)}) collective-permute-start(s32[2,6]{1,0:T(2,128)} %bitcast.147), channel_id=1, source_target_pairs={{0,192},{64,0},{128,64},{192,128},{1,193},{65,1},{129,65},{193,129... | collective-permute-start | bytes 152 | tf_op jit(solution)/shard_map/ppermute | solution.py:20
  4.0 0.9 slice_bitcast_fusion
  4.9 1.3 collective-permute-start.2
  6.3 0.8 reshape_squeeze.3
  7.0 0.7 broadcast_add_fusion
  7.7 0.7 fusion.46
  8.4 0.6 fusion.48
  9.0 0.8 slice_bitcast_fusion.24
  9.8 1.0 fusion.52
  10.7 2.7 fusion.53
  13.4 0.6 slice.314
  14.1 0.6 slice.317
  14.7 0.8 bitcast_select_fusion
  15.4 0.5 slice_bitcast_fusion.19
  16.0 0.7 mul.584
  16.9 0.6 slice_bitcast_fusion.12
  17.5 0.6 slice_bitcast_fusion.6
  18.1 0.6 slice_bitcast_fusion.22
  19.1 0.6 pad.21.clone
  19.8 0.6 concatenate.29.g2
  20.5 2.6 convolution_convert_fusion
  23.1 0.9 convolution_add_fusion
  24.2 0.9 multiply_reduce_fusion.1
  25.1 0.8 concatenate.28
  25.9 0.6 scatter.4.meta
  26.5 0.9 pad_maximum_fusion.1
  27.9 2.5 fusion.12
  30.4 0.5 add_rsqrt_fusion
  31.3 0.7 slice_multiply_fusion.1
  32.1 0.9 maximum_maximum_fusion
  33.5 0.6 collective-permute-start.3
  34.1 0.9 maximum_bitcast_fusion.pk
  34.9 208.9 %expert_chain.1 = (bf16[2,3,448,512]{3,2,1,0:T(8,128)(2,1)}, bf16[2,16,16,448]{3,2,1,0:T(8,128)(2,1)}) custom-call(bf16[2,16,16,448]{3,2,1,0:T(8,128)(2,1)} %maximum_bitcast_fusion.pk, f32[8,128]{1,0:T(8,128)} %scatter.4.meta, f32[8,448]{1,0:T(8,128)} %concatenate.29.g2, bf16[2,3,448,512]{3,2,1,0:T(8,128)(2,1)} %w.1), custom_call_target="tpu_custom_call" | custom-call | flops 4000000000 | bytes 150000000 | tf_op jit(solution)/shard_map/expert_chain/pallas_call | solution.py:387
  243.8 1.2 convert_bitcast_fusion
  245.1 0.6 copy.13
  245.7 1.3 reshape.190
  247.0 3.6 %fusion.51 = (f32[1,1,7168]{2,1,0:T(1,128)S(1)}, f32[1,1,7168]{2,1,0:T(1,128)S(1)}, f32[1,1,7168]{2,1,0:T(1,128)S(1)}, f32[1,1,7168]{2,1,0:T(1,128)S(1)}, f32[1,...) fusion(f32[2,16,7168]{2,1,0:T(8,128)} %reshape.190), kind=kLoop, calls=%fused_computation.123 | loop fusion | bytes 1032192 | tf_op jit(solution)/shard_map/slice | solution.py:479
  251.3 4.8 %fusion.18 = (f32[128]{0:T(128)S(1)}, bf16[128,7168]{1,0:T(8,128)(2,1)S(1)}) fusion(f32[7168]{0:T(1024)S(1)} %bitcast.139, f32[128]{0:T(128)S(1)} %copy-done.23, f32[7168]{0:T(1024)S(1)} %bitcast.140, f32[128]{0:T(128)S(1)} %copy-done.24, f32[7168]{0:T(1024)S(1)} %bitcast.141, f32[128]{0:T(128)S(1)} %copy-done.25, f32[7168]{0:T(1024)S(1)} %bitcast.142, ...), kind=kLoop, calls=%fused_computation.28 | loop fusion | flops 22937472 | bytes 5739008 | tf_op jit(solution)/shard_map/reduce_sum | solution.py:31
  256.2 4.2 %fusion.17 = (f32[7168]{0:T(1024)S(1)}, f32[128]{0:T(128)S(1)}, f32[7168]{0:T(1024)S(1)}, f32[128,7168]{1,0:T(8,128)S(1)}) fusion(bf16[128,7168]{1,0:T(8,128)(2,1)S(1)} %get-tuple-element.32, f32[128]{0:T(128)S(1)} %add_rsqrt_fusion.1, f32[7168]{0:T(1024)S(1)} %bitcast.123, f32[128]{0:T(128)S(1)} %copy-done.28, ...), kind=kLoop, calls=%fused_computation.27 | loop fusion | flops 24758144 | bytes 9466368 | tf_op jit(solution)/shard_map/reduce_sum | solution.py:541
  260.5 6.6 %fusion.26 = (f32[7168]{0:T(1024)S(1)}, f32[128]{0:T(128)S(1)}, f32[7168]{0:T(1024)S(1)}, f32[128,7168]{1,0:T(8,128)S(1)}) fusion(bf16[1,1,128,7168]{3,2,1,0:T(8,128)(2,1)S(1)} %collective-permute-done.3, f32[128]{0:T(128)S(1)} %add_rsqrt_fusion.3, f32[7168]{0:T(1024)S(1)} %bitcast.121, f32[128]{0:T(128)S(1)} %copy-done.8, ...), kind=kLoop, calls=%fused_computation.36 | loop fusion | flops 26593152 | bytes 13137408 | tf_op jit(solution)/shard_map/reduce_sum | solution.py:544
  267.1 2.1 fusion.29
  269.2 3.0 collective-permute-start.4
  272.7 0.7 concatenate.31.parts
  273.4 21.2 %gain_sum.1 = f32[8,448]{1,0:T(8,128)} custom-call(f32[16,8,448]{2,1,0:T(8,128)} %concatenate.31.parts), custom_call_target="tpu_custom_call" | custom-call | flops 1000000 | bytes 30000000 | tf_op jit(solution)/shard_map/gain_sum/pallas_call | solution.py:452
  294.6 1.4 constant_dynamic-slice_fusion
  296.0 16.1 %collective-permute-done.4 = bf16[1,1,128,7168]{3,2,1,0:T(8,128)(2,1)} collective-permute-done((bf16[1,1,128,7168]{3,2,1,0:T(8,128)(2,1)}, bf16[1,1,128,7168]{3,2,1,0:T(8,128)(2,1)}, u32[]{:S(2)}, u32[]{:S(2)}) %collective-permute-start.4) | collective-permute-done | bytes 1835040 | tf_op jit(solution)/shard_map/ppermute | solution.py:20
  312.0 2.8 copy.16
  314.9 1.5 copy.17
  (98 shorter events, 3.4 us)
Async XLA Ops:
  0.6 18.1 %copy-start = (bf16[1,1,128,7168]{3,2,1,0:T(8,128)(2,1)S(1)}, bf16[1,1,128,7168]{3,2,1,0:T(8,128)(2,1)}, u32[]{:S(2)}) copy-start(bf16[1,1,128,7168]{3,2,1,0:T(8,128)(2,1)} %param.11) | copy-start | bytes 5505028
  0.6 19.1 %slice-start = ((f32[2,2,7168]{2,1,0:T(2,128)}), f32[1,2,7168]{2,1,0:T(2,128)S(1)}, s32[]{:S(2)}) async-start(f32[2,2,7168]{2,1,0:T(2,128)} %param.16), calls=%async_computation | async-start | bytes 114688 | tf_op jit(solution)/shard_map/slice | solution.py:526
  0.7 19.7 %collective-permute-start = (s32[2,6]{1,0:T(2,128)}, s32[2,6]{1,0:T(2,128)S(1)}, u32[]{:S(2)}, u32[]{:S(2)}) collective-permute-start(s32[2,6]{1,0:T(2,128)} %bitcast.147), channel_id=1, source_target_pairs={{0,192},{64,0},{128,64},{192,128},{1,193},{65,1},{129,65},{193,129... | collective-permute-start | bytes 152 | tf_op jit(solution)/shard_map/ppermute | solution.py:20
  4.9 18.2 %collective-permute-start.2 = (bf16[2,7168]{1,0:T(2,128)(2,1)S(1)}, bf16[2,7168]{1,0:T(2,128)(2,1)S(1)}, u32[]{:S(2)}, u32[]{:S(2)}) collective-permute-start(bf16[2,7168]{1,0:T(2,128)(2,1)S(1)} %slice_bitcast_fusion), channel_id=1, source_target_pairs={{4,0},{8,4},{12,8},{16,12},{20,16},{24,20},{28,24},{32,28},{36,32}... | collective-permute-start | bytes 86024 | tf_op jit(solution)/shard_map/ppermute | solution.py:26
  9.0 11.5 %copy-start.7 = (f32[6]{0:T(128)}, f32[6]{0:T(128)S(1)}, u32[]{:S(2)}) copy-start(f32[6]{0:T(128)S(1)} %get-tuple-element.82) | copy-start | bytes 76
  15.9 4.5 %copy-start.9 = (f32[6]{0:T(128)}, f32[6]{0:T(128)S(1)}, u32[]{:S(2)}) copy-start(f32[6]{0:T(128)S(1)} %get-tuple-element.83) | copy-start | bytes 76
  16.8 3.6 %copy-start.6 = (pred[18,130]{1,0:T(8,128)(4,1)}, pred[18,130]{1,0:T(8,128)(4,1)S(1)}, u32[]{:S(2)}) copy-start(pred[18,130]{1,0:T(8,128)(4,1)S(1)} %iota_compare_fusion) | copy-start | bytes 7024
  20.5 3.8 %copy-start.5 = (f32[12,7168]{1,0:T(8,128)S(1)}, f32[12,7168]{1,0:T(8,128)}, u32[]{:S(2)}) copy-start(f32[12,7168]{1,0:T(8,128)} %get-tuple-element.88) | copy-start | bytes 1032196
  20.5 3.8 %copy-start.29 = (f32[6]{0:T(128)S(1)}, f32[6]{0:T(128)}, u32[]{:S(2)}) copy-start(f32[6]{0:T(128)} %get-tuple-element.84) | copy-start | bytes 76
  23.1 7.8 %collective-permute-start.1 = (bf16[12,7168]{1,0:T(8,128)(2,1)}, bf16[12,7168]{1,0:T(8,128)(2,1)S(1)}, u32[]{:S(2)}, u32[]{:S(2)}) collective-permute-start(bf16[12,7168]{1,0:T(8,128)(2,1)} %convolution_convert_fusion), channel_id=1, source_target_pairs={{0,64},{64,128},{128,192},{192,0},{1,65},{65,129},{129,193},{193,1... | collective-permute-start | bytes 516104 | tf_op jit(solution)/shard_map/ppermute | solution.py:20
  33.5 217.3 %collective-permute-start.3 = (bf16[1,1,128,7168]{3,2,1,0:T(8,128)(2,1)}, bf16[1,1,128,7168]{3,2,1,0:T(8,128)(2,1)S(1)}, u32[]{:S(2)}, u32[]{:S(2)}) collective-permute-start(bf16[1,1,128,7168]{3,2,1,0:T(8,128)(2,1)} %param.10), channel_id=1, source_target_pairs={{0,64},{64,128},{128,192},{192,0},{1,65},{65,129},{129,193},{193,1... | collective-permute-start | bytes 5505032 | tf_op jit(solution)/shard_map/ppermute | solution.py:20
  245.0 6.2 %copy-start.8 = (f32[128]{0:T(128)S(1)}, f32[128]{0:T(128)}, u32[]{:S(2)}) copy-start(f32[128]{0:T(128)} %get-tuple-element.90) | copy-start | bytes 1540
  245.0 6.2 %copy-start.22 = (f32[128]{0:T(128)S(1)}, f32[128]{0:T(128)}, u32[]{:S(2)}) copy-start(f32[128]{0:T(128)} %get-tuple-element.67) | copy-start | bytes 1540
  245.0 6.2 %copy-start.23 = (f32[128]{0:T(128)S(1)}, f32[128]{0:T(128)}, u32[]{:S(2)}) copy-start(f32[128]{0:T(128)} %get-tuple-element.68) | copy-start | bytes 1540
  245.0 6.2 %copy-start.24 = (f32[128]{0:T(128)S(1)}, f32[128]{0:T(128)}, u32[]{:S(2)}) copy-start(f32[128]{0:T(128)} %get-tuple-element.69) | copy-start | bytes 1540
  245.0 6.2 %copy-start.25 = (f32[128]{0:T(128)S(1)}, f32[128]{0:T(128)}, u32[]{:S(2)}) copy-start(f32[128]{0:T(128)} %get-tuple-element.70) | copy-start | bytes 1540
  245.0 6.2 %copy-start.26 = (f32[128]{0:T(128)S(1)}, f32[128]{0:T(128)}, u32[]{:S(2)}) copy-start(f32[128]{0:T(128)} %get-tuple-element.71) | copy-start | bytes 1540
  245.1 6.2 %copy-start.27 = (f32[128]{0:T(128)S(1)}, f32[128]{0:T(128)}, u32[]{:S(2)}) copy-start(f32[128]{0:T(128)} %get-tuple-element.72) | copy-start | bytes 1540
  247.0 4.2 %copy-start.2 = (bf16[128,7168]{1,0:T(8,128)(2,1)S(1)}, bf16[128,7168]{1,0:T(8,128)(2,1)}, u32[]{:S(2)}) copy-start(bf16[128,7168]{1,0:T(8,128)(2,1)} %get-tuple-element.34) | copy-start | bytes 5505028
  250.6 5.4 %copy-start.1 = (bf16[1,1,128,7168]{3,2,1,0:T(8,128)(2,1)S(1)}, bf16[1,1,128,7168]{3,2,1,0:T(8,128)(2,1)}, u32[]{:S(2)}) copy-start(bf16[1,1,128,7168]{3,2,1,0:T(8,128)(2,1)} %param.11) | copy-start | bytes 5505028
  250.6 5.4 %copy-start.3 = (bf16[1,1,128,7168]{3,2,1,0:T(8,128)(2,1)S(1)}, bf16[1,1,128,7168]{3,2,1,0:T(8,128)(2,1)}, u32[]{:S(2)}) copy-start(bf16[1,1,128,7168]{3,2,1,0:T(8,128)(2,1)} %param.12) | copy-start | bytes 5505028
  250.7 5.4 %copy-start.16 = (f32[128]{0:T(128)S(1)}, f32[128]{0:T(128)}, u32[]{:S(2)}) copy-start(f32[128]{0:T(128)} %get-tuple-element.61) | copy-start | bytes 1540
  250.7 5.4 %copy-start.17 = (f32[128]{0:T(128)S(1)}, f32[128]{0:T(128)}, u32[]{:S(2)}) copy-start(f32[128]{0:T(128)} %get-tuple-element.62) | copy-start | bytes 1540
  250.7 5.4 %copy-start.18 = (f32[128]{0:T(128)S(1)}, f32[128]{0:T(128)}, u32[]{:S(2)}) copy-start(f32[128]{0:T(128)} %get-tuple-element.63) | copy-start | bytes 1540
  250.7 5.4 %copy-start.19 = (f32[128]{0:T(128)S(1)}, f32[128]{0:T(128)}, u32[]{:S(2)}) copy-start(f32[128]{0:T(128)} %get-tuple-element.64) | copy-start | bytes 1540
  250.7 5.4 %copy-start.20 = (f32[128]{0:T(128)S(1)}, f32[128]{0:T(128)}, u32[]{:S(2)}) copy-start(f32[128]{0:T(128)} %get-tuple-element.65) | copy-start | bytes 1540
  250.7 5.4 %copy-start.21 = (f32[128]{0:T(128)S(1)}, f32[128]{0:T(128)}, u32[]{:S(2)}) copy-start(f32[128]{0:T(128)} %get-tuple-element.66) | copy-start | bytes 1540
  250.7 5.4 %copy-start.28 = (f32[128]{0:T(128)S(1)}, f32[128]{0:T(128)}, u32[]{:S(2)}) copy-start(f32[128]{0:T(128)} %get-tuple-element.89) | copy-start | bytes 1540
  256.1 4.3 %copy-start.10 = (f32[128]{0:T(128)S(1)}, f32[128]{0:T(128)}, u32[]{:S(2)}) copy-start(f32[128]{0:T(128)} %get-tuple-element.73) | copy-start | bytes 1540
  256.1 4.3 %copy-start.11 = (f32[128]{0:T(128)S(1)}, f32[128]{0:T(128)}, u32[]{:S(2)}) copy-start(f32[128]{0:T(128)} %get-tuple-element.74) | copy-start | bytes 1540
  256.1 4.3 %copy-start.12 = (f32[128]{0:T(128)S(1)}, f32[128]{0:T(128)}, u32[]{:S(2)}) copy-start(f32[128]{0:T(128)} %get-tuple-element.75) | copy-start | bytes 1540
  256.2 4.3 %copy-start.13 = (f32[128]{0:T(128)S(1)}, f32[128]{0:T(128)}, u32[]{:S(2)}) copy-start(f32[128]{0:T(128)} %get-tuple-element.76) | copy-start | bytes 1540
  256.2 4.3 %copy-start.14 = (f32[128]{0:T(128)S(1)}, f32[128]{0:T(128)}, u32[]{:S(2)}) copy-start(f32[128]{0:T(128)} %get-tuple-element.77) | copy-start | bytes 1540
  256.2 4.3 %copy-start.15 = (f32[128]{0:T(128)S(1)}, f32[128]{0:T(128)}, u32[]{:S(2)}) copy-start(f32[128]{0:T(128)} %get-tuple-element.78) | copy-start | bytes 1540
  269.2 45.7 %copy-start.4 = (bf16[2,3,448,512]{3,2,1,0:T(8,128)(2,1)S(1)}, bf16[2,3,448,512]{3,2,1,0:T(8,128)(2,1)}, u32[]{:S(2)}) copy-start(bf16[2,3,448,512]{3,2,1,0:T(8,128)(2,1)} %get-tuple-element.22) | copy-start | bytes 8257540
  269.2 42.8 %collective-permute-start.4 = (bf16[1,1,128,7168]{3,2,1,0:T(8,128)(2,1)}, bf16[1,1,128,7168]{3,2,1,0:T(8,128)(2,1)}, u32[]{:S(2)}, u32[]{:S(2)}) collective-permute-start(bf16[1,1,128,7168]{3,2,1,0:T(8,128)(2,1)} %fusion.29), channel_id=1, source_target_pairs={{0,192},{64,0},{128,64},{192,128},{1,193},{65,1},{129,65},{193,129... | collective-permute-start | bytes 5505032 | tf_op jit(solution)/shard_map/ppermute | solution.py:20

commit v2 on v1

--- a/solution.py
+++ b/solution.py
@@ -97,7 +97,7 @@
             lax.fori_loop(1, size, body, 0)
 
 
-def greet(axes):
+def greet(axes, sections=()):
     barrier = pltpu.get_barrier_semaphore()
     total = 0
     for axis, size, me in axes:
@@ -109,13 +109,19 @@
 
         lax.fori_loop(1, size, body, 0)
         total += size - 1
+    for to in sections:
+        pl.semaphore_signal(barrier, inc=1, device_id={"section": to}, device_id_type=MESH)
+        total += 1
     pl.semaphore_wait(barrier, total)
 
 
-def chain_kernel(S, Q, C, D, pk, meta, g2, w, eg, ret, land, mland, rows, xr, do, gu, lg, da, ld,
-                 act, dg, op, lo, pv, ss, ssl, od, rb, gsv, send, recv):
+def chain_kernel(S, Q, X, C, D, pk, meta, slots, g2, w, mh, ext, cot, sl, ng, eg, hg, slr, gains,
+                 ret, land, mland, rows, xr, do, gu, lg, da, ld, act, dg, op, lo, pv, ss, ssl, od, rb, gsv,
+                 hid, hgs, es, mx, dmx, ad, sls, gacc, gsrc, gland, gown, gland2, send, recv, xsend, xrecv):
     me = lax.axis_index("seq")
     d = lax.axis_index("dp")
+    sec = lax.axis_index("section")
+    after, before_me = lax.rem(sec + 1, X), lax.rem(sec + X - 1, X)
     DS, HS = w.shape[2], w.shape[3]
     RW = C * S
     CG = S // Q
@@ -143,7 +149,33 @@
     def dp_wait(ph, dst_of):
         wires.wait(ph, "dp", Q, d, dst_of)
 
-    greet((("seq", S, me), ("dp", Q, d)))
+    greet((("seq", S, me), ("dp", Q, d)), (after, before_me))
+
+    NC = mh.shape[0] // PK
+
+    def chunk(c):
+        return pl.ds(pl.multiple_of(c * PK, PK), PK)
+
+    def hop(src, dst, slot, to):
+        return pltpu.make_async_remote_copy(
+            src_ref=src, dst_ref=dst, send_sem=xsend.at[slot], recv_sem=xrecv.at[slot],
+            device_id={"section": to}, device_id_type=MESH,
+        )
+
+    def hid_copy(c):
+        return hop(mh.at[chunk(c), :], hid.at[chunk(c), :], c, after)
+
+    def hg_copy(c):
+        return hop(hgs.at[chunk(c), :], hg.at[chunk(c), :], NC + c, before_me)
+
+    def each_chunk(fn, first=0, last=NC):
+        def body(c, carry):
+            fn(c)
+            return carry
+
+        lax.fori_loop(first, last, body, 0)
+
+    each_chunk(lambda c: hid_copy(c).start())
 
     def blk(b):
         return pl.ds(pl.multiple_of(b * PK, PK), PK)
@@ -258,6 +290,137 @@
     def down_grad(k):
         for q in range(CG):
             eg[k, 2, :, q * PC:(q + 1) * PC] = dot_tn(do[k], act[k, q, 0]).astype(BF16)
+
+    LB = 256
+    NB = D // LB
+
+    def lanes(b):
+        return pl.ds(pl.multiple_of(b * LB, LB), LB)
+
+    def sweep(fn, count):
+        zero = jnp.zeros((PK, LB), F32)
+        total = lax.fori_loop(0, NB, lambda b, acc: fn(lanes(b), acc), (zero,) * count)
+        return [jnp.sum(t, axis=1, keepdims=True) * (1.0 / D) for t in total]
+
+    def gain(k, at):
+        return ng[k:k + 1, at]
+
+    def collect(k, at, value, mask):
+        value = value * mask
+        gacc[k, :, at] += value[:8] + value[8:]
+
+    def rows_pass_1(h_at, e_at, c_at, mask, prev_add, dm2_add):
+        def squares(at, acc):
+            h, e1, e2 = h_at(at), e_at(0, at), e_at(1, at)
+            return acc[0] + h * h, acc[1] + e1 * e1, acc[2] + e2 * e2
+
+        sh, se1, se2 = [lax.rsqrt(v + eps_norm) for v in sweep(squares, 3)]
+
+        def mix(at, acc):
+            m = (h_at(at) * sh) * gain(0, at) + (e_at(0, at) * se1) * gain(1, at)
+            m = m.astype(BF16).astype(F32)
+            if prev_add is not None:
+                m = (m + prev_add(at)).astype(BF16).astype(F32)
+            mx[:, at] = m
+            return (acc[0] + m * m,)
+
+        s2, = [lax.rsqrt(v + eps_norm) for v in sweep(mix, 1)]
+
+        def top(at, acc):
+            n2 = mx[:, at] * s2
+            dm2 = c_at(at)
+            if dm2_add is not None:
+                dm2 = dm2 + dm2_add(at)
+            collect(2, at, dm2 * n2, mask)
+            collect(3, at, dm2 * (e_at(1, at) * se2), mask)
+            u = dm2 * gain(2, at)
+            dmx[:, at] = u
+            return (acc[0] + u * n2,)
+
+        inner, = sweep(top, 1)
+
+        def middle(at, acc):
+            dmx[:, at] = (dmx[:, at] - (mx[:, at] * s2) * inner) * s2
+            return acc
+
+        sweep(middle, 0)
+        return sh, se1
+
+    def rows_pass_2(h_at, e_at, mask, sh, se1, dm1_add, store):
+        def low(at, acc):
+            dm1 = dmx[:, at]
+            if dm1_add is not None:
+                dm1 = dm1 + dm1_add(at)
+            n1 = h_at(at) * sh
+            collect(0, at, dm1 * n1, mask)
+            collect(1, at, dm1 * (e_at(0, at) * se1), mask)
+            u = dm1 * gain(0, at)
+            dmx[:, at] = u
+            return (acc[0] + u * n1,)
+
+        inner, = sweep(low, 1)
+
+        def last(at, acc):
+            store(at, ((dmx[:, at] - (h_at(at) * sh) * inner) * sh).astype(BF16))
+            return acc
+
+        sweep(last, 0)
+
+    slot_row, live_row, weight_row, fresh_row = (slots[k:k + 1, :] for k in range(4))
+    lane16 = lax.broadcasted_iota(jnp.int32, (PK, 128), 1)
+    line16 = lax.broadcasted_iota(jnp.int32, (PK, 128), 0)
+
+    def column(row):
+        return jnp.sum(jnp.where(lane16 == line16, row, 0.0), axis=1, keepdims=True)
+
+    def bulk_chunk(c):
+        hid_copy(c).wait_recv()
+        r = lax.broadcasted_iota(jnp.int32, (2 * PK, 2 * PK), 0)
+        k = lax.broadcasted_iota(jnp.int32, (2 * PK, 2 * PK), 1)
+        shift = jnp.where(k == r % PK + 1 + r // PK, 1.0, 0.0).astype(BF16)
+        es[...] = dot_nn(shift, ext[pl.ds(pl.multiple_of(c * PK, PK), 2 * PK), :]).astype(BF16)
+        place = (line16 + c * PK).astype(F32)
+        hit = jnp.sum(jnp.where(place == slot_row, live_row, 0.0), axis=1, keepdims=True)
+        mask = jnp.where(hit > 0.5, 0.0, 1.0)
+
+        def h_at(at):
+            return hid[chunk(c), at].astype(F32)
+
+        def e_at(k, at):
+            return es[k * PK:(k + 1) * PK, at].astype(F32)
+
+        sh, se1 = rows_pass_1(h_at, e_at, lambda at: cot[chunk(c), at].astype(F32), mask, None, None)
+
+        def store(at, value):
+            hgs[chunk(c), at] = value
+
+        rows_pass_2(h_at, e_at, mask, sh, se1, None, store)
+        hg_copy(c).start()
+
+    def bulk(first, last):
+        each_chunk(bulk_chunk, first, last)
+
+    gacc[...] = jnp.zeros_like(gacc)
+
+    def slot_h(at):
+        return sl[0, :, at].astype(F32)
+
+    def slot_e(k, at):
+        return sl[1 + k, :, at].astype(F32)
+
+    slot_mask = column(fresh_row)
+    slot_tok = column(slot_row)
+    same_tok = jnp.where(slot_tok == slot_row, live_row, 0.0)
+    prev_sel = jnp.where(lane16 < C, same_tok, 0.0)
+    prev_w = jnp.sum(prev_sel * weight_row, axis=1, keepdims=True)
+    dm2_sel = jnp.where((lane16 >= C) & (lane16 < 2 * C), same_tok, 0.0)
+
+    def widen(n, sel, k, scale_by):
+        for b in range(S):
+            part = dot_nn(sel[:, :PK].astype(BF16), ret[k, b])
+            if scale_by is not None:
+                part = part * scale_by
+            ad[n, :, b * DS:(b + 1) * DS] = part
 
     seq_wait(ph_b, lambda frm: land.at[0, blk(frm), :])
     unpack(0)
@@ -273,6 +436,7 @@
     gsv[0] = gate_up_wait(ph, 0)
     act_piece(0)
     ph = spread_piece(act.at[0])
+    bulk(0, 3 * NC // 8)
     spread_wait(ph, act.at[0])
     out = None
     for q in range(CG):
@@ -280,6 +444,7 @@
         out = part if out is None else out + part
     ph = reduce_dp(0, out)
     ph_da2 = dact(1)
+    bulk(3 * NC // 8, NC // 2)
     seq_wait(ph_m, lambda frm: mland.at[frm])
     facts = jnp.sum(mland[...], axis=1)
 
@@ -316,6 +481,7 @@
     ph = gather_dp(1, xr)
     gather_dp_wait(ph, 1, xr)
     ph = gate_up(1)
+    bulk(NC // 2, NC)
     d_act = dact_wait(ph_da2, 1)
     gsv[1] = gate_up_wait(ph, 1)
     pre_grads(1, d_act)
@@ -364,35 +530,74 @@
     pre_grads(0, d_act)
     ph = spread_piece(dg.at[0])
     ph_r0 = send_back(0, 0, 2 * RW)
+    seq_wait(ph_r0, lambda frm: ret.at[0, frm])
+    widen(0, prev_sel, 0, prev_w)
+    widen(1, dm2_sel, 0, None)
+    slot_sh, slot_se1 = rows_pass_1(
+        slot_h, slot_e, lambda at: sl[3, :, at].astype(F32), slot_mask, lambda at: ad[0, :, at], lambda at: ad[1, :, at]
+    )
     spread_wait(ph, dg.at[0])
     ph = reduce_dp(2, drows(0))
     in_grads(0)
     back = reduce_dp_wait(ph, 2)
     od[2 * RW:3 * RW, :] = back.astype(BF16)
     ph_r1 = send_back(1, 2 * RW, 3 * RW)
-    seq_wait(ph_r0, lambda frm: ret.at[0, frm])
     seq_wait(ph_r1, lambda frm: ret.at[1, frm])
+    widen(2, prev_sel, 1, None)
+
+    def slot_store(at, value):
+        sls[:, at] = value
+
+    rows_pass_2(slot_h, slot_e, slot_mask, slot_sh, slot_se1, lambda at: ad[2, :, at], slot_store)
+    back_rows = hop(sls, slr, 2 * NC, before_me)
+    back_rows.start()
+
+    for b in range(S):
+        part = gacc[:, :, b * DS:(b + 1) * DS]
+        gsrc[b] = jnp.sum(part, axis=1)
+    ph = seq_start(lambda to: gsrc.at[to], gland.at[me])
+    gland[me] = gsrc[me]
+    seq_wait(ph, lambda frm: gland.at[frm])
+    value = add_up(gland)
+    gown[...] = value
+    ph = dp_start(lambda to: gown, gland2.at[d])
+    gland2[d] = value
+    dp_wait(ph, lambda frm: gland2.at[frm])
+    gains[...] = add_up(gland2)
+
+    def finish(c):
+        hid_copy(c).wait_send()
+        hg_copy(c).wait_send()
+        hg_copy(c).wait_recv()
+
+    each_chunk(finish)
+    back_rows.wait()
     wires.drain()
 
 
-def chain(pk, meta, g2, w, C, D):
-    S, Q = lax.axis_size("seq"), lax.axis_size("dp")
+def chain(pk, meta, slots, g2, w, mh, ext, cot, sl, ng, C):
+    S, Q, X = lax.axis_size("seq"), lax.axis_size("dp"), lax.axis_size("section")
     DS, HS = w.shape[2], w.shape[3]
+    T, D = mh.shape
     RW = C * S
     NR = Q * RW
     CG = S // Q
     PC = HS // CG
+    NC = T // PK
     vm = pltpu.VMEM
     phases = 24
     return pl.pallas_call(
-        functools.partial(chain_kernel, S, Q, C, D),
+        functools.partial(chain_kernel, S, Q, X, C, D),
         out_shape=(
             jax.ShapeDtypeStruct(w.shape, BF16),
-            jax.ShapeDtypeStruct((2, S, PK, DS), BF16),
+            jax.ShapeDtypeStruct((T, D), BF16),
+            jax.ShapeDtypeStruct((PK, D), BF16),
+            jax.ShapeDtypeStruct((4, DS), F32),
         ),
-        in_specs=[pl.BlockSpec(memory_space=vm)] * 4,
-        out_specs=(pl.BlockSpec(memory_space=vm),) * 2,
+        in_specs=[pl.BlockSpec(memory_space=vm)] * 10,
+        out_specs=(pl.BlockSpec(memory_space=vm),) * 4,
         scratch_shapes=[
+            vm((2, S, PK, DS), BF16),
             vm((2, S * PK, DS), BF16),
             vm((S, 8, 128), F32),
             vm((2, S * PK, DS), F32),
@@ -412,73 +617,32 @@
             vm((3 * RW, DS), BF16),
             vm((2, S * PK, DS), BF16),
             vm((2, 2, RW, PC), F32),
+            vm((T, D), BF16),
+            vm((T, D), BF16),
+            vm((2 * PK, D), BF16),
+            vm((PK, D), F32),
+            vm((PK, D), F32),
+            vm((3, PK, D), F32),
+            vm((PK, D), BF16),
+            vm((4, 8, D), F32),
+            vm((S, 4, DS), F32),
+            vm((S, 4, DS), F32),
+            vm((4, DS), F32),
+            vm((Q, 4, DS), F32),
             pltpu.SemaphoreType.DMA((phases, S)),
             pltpu.SemaphoreType.DMA((phases, S)),
+            pltpu.SemaphoreType.DMA((2 * NC + 1,)),
+            pltpu.SemaphoreType.DMA((2 * NC + 1,)),
         ],
         compiler_params=pltpu.CompilerParams(
-            collective_id=0, has_side_effects=True, vmem_limit_bytes=56 * 1024 * 1024
+            collective_id=0, has_side_effects=True, vmem_limit_bytes=60 * 1024 * 1024
         ),
-        cost_estimate=pl.CostEstimate(flops=4 * 10**9, bytes_accessed=150 * 10**6, transcendentals=10**6),
         name="expert_chain",
-    )(pk, meta, g2, w)
-
-
-def gain_kernel(S, Q, parts, total, land, mine, land2, send, recv):
-    me = lax.axis_index("seq")
-    d = lax.axis_index("dp")
-    wires = Wires(send, recv)
-    greet((("seq", S, me), ("dp", Q, d)))
-    ph = wires.start("seq", S, me, lambda to: parts.at[to], land.at[me])
-    land[me] = parts[me]
-    wires.wait(ph, "seq", S, me, lambda frm: land.at[frm])
-    value = land[0]
-    for b in range(1, S):
-        value = value + land[b]
-    mine[...] = value
-    ph = wires.start("dp", Q, d, lambda to: mine, land2.at[d])
-    land2[d] = value
-    wires.wait(ph, "dp", Q, d, lambda frm: land2.at[frm])
-    value = land2[0]
-    for b in range(1, Q):
-        value = value + land2[b]
-    total[...] = value
-    wires.drain()
-
-
-def gain_sum(parts):
-    S, Q = lax.axis_size("seq"), lax.axis_size("dp")
-    shape = parts.shape[1:]
-    vm = pltpu.VMEM
-    return pl.pallas_call(
-        functools.partial(gain_kernel, S, Q),
-        out_shape=jax.ShapeDtypeStruct(shape, F32),
-        in_specs=[pl.BlockSpec(memory_space=vm)],
-        out_specs=pl.BlockSpec(memory_space=vm),
-        scratch_shapes=[
-            vm((S,) + shape, F32),
-            vm(shape, F32),
-            vm((Q,) + shape, F32),
-            pltpu.SemaphoreType.DMA((2, S)),
-            pltpu.SemaphoreType.DMA((2, S)),
-        ],
-        compiler_params=pltpu.CompilerParams(collective_id=1, has_side_effects=True),
-        cost_estimate=pl.CostEstimate(flops=10**6, bytes_accessed=30 * 10**6, transcendentals=0),
-        name="gain_sum",
-    )(parts)
+    )(pk, meta, slots, g2, w, mh, ext, cot, sl, ng)
 
 
 def pick(index, count):
     return (index[:, None] == jnp.arange(count, dtype=jnp.int32)[None, :]).astype(BF16)
-
-
-def put_rows(tokens, rows, weight, count):
-    at = (jnp.arange(count, dtype=jnp.int32)[:, None] == tokens[None, :]).astype(F32)
-    at = at * weight[None, :]
-    total = None
-    for i in range(rows.shape[0]):
-        part = at[:, i:i + 1] * rows[i:i + 1]
-        total = part if total is None else total + part
-    return total
 
 
 def local(main_hidden, embedded, cotangent, slot_token, slot_count, route_gate, norm_gain, w):
@@ -490,24 +654,25 @@
     tok = slot_token[0, 0]
     live = (jnp.arange(C, dtype=jnp.int32)[None, :] < slot_count[0, 0]).astype(F32)
     weight = route_gate[0, 0] * live
-    own, cot = embedded[0, 0], cotangent[0, 0]
+    own, cot, mh = embedded[0, 0], cotangent[0, 0], main_hidden[0, 0]
     ahead = from_ahead(own[:2], "seq", 1)
-
-    asked = from_behind(tok, "section", -1).reshape(-1)
-    sent = dot_nn(pick(asked, tokens_here), main_hidden[0, 0]).astype(BF16)
+    same = (tok[1][:, None] == tok[0][None, :]).astype(F32) * live[1][:, None] * live[0][None, :]
+    fresh = jnp.stack([live[0], live[1] * (1.0 - jnp.max(same, axis=1))]).reshape(-1)
+    flat = tok.reshape(-1)
+    merge = jnp.where(fresh > 0.5, flat, -1)
+
+    asked, back_to = from_behind(jnp.stack([flat, merge]), "section", -1)
+    sent = dot_nn(pick(asked, tokens_here), mh).astype(BF16)
     h_rows = from_behind(sent, "section", 1)
-    bulk, h_rows = lax.optimization_barrier((main_hidden, h_rows))
-    hidden = from_behind(bulk, "section", 1)[0, 0]
-
-    flat = tok.reshape(-1)
-    places = jnp.concatenate([flat + 1, tok[1] + 2])
+
+    places = jnp.concatenate([flat + 1, flat + 2])
     e_pick = pick(places, tokens_here + 2)
     e_rows = dot_nn(e_pick[:, :tokens_here], own) + dot_nn(e_pick[:, tokens_here:], ahead)
     c_rows = dot_nn(pick(flat, tokens_here), cot)
     unit_h, _ = normed(h_rows)
     unit_e, _ = normed(e_rows[:2 * C])
     mixed = (unit_h * norm_gain[0, 0] + unit_e * norm_gain[0, 1]).astype(BF16)
-    e2 = e_rows[2 * C:]
+    e2 = e_rows[3 * C:]
     _, se2 = normed(e2)
     m1 = mixed[:C] * live[0][:, None].astype(BF16)
     e2 = (e2 * live[1][:, None]).astype(BF16)
@@ -518,40 +683,30 @@
     pk_b = jnp.concatenate([m1, mixed[C:], c1[cut:], pad], 0)
     pk_a = jnp.concatenate([e2, dout2, c1[:cut]], 0)
     pk = jnp.stack([pk_b, pk_a]).reshape(2, PK, S, DS).transpose(0, 2, 1, 3)
-    same = (tok[1][:, None] == tok[0][None, :]).astype(F32) * live[1][:, None] * live[0][None, :]
     facts = jnp.concatenate(
         [weight[0], jnp.zeros((8 - C,), F32), se2[:, 0], jnp.zeros((8 - C,), F32), same.reshape(-1)]
     )
-    meta = jnp.zeros((8, 128), F32).at[0, :facts.shape[0]].set(facts)
+    meta = jnp.pad(facts[None, :], ((0, 7), (0, 128 - facts.shape[0])))
+    slots = jnp.stack([flat.astype(F32), live.reshape(-1), weight.reshape(-1), fresh])
+    slots = jnp.pad(slots, ((0, 4), (0, 128 - 2 * C)))
     g2 = lax.dynamic_slice(norm_gain[1], (0, me * DS), (2, DS))
     g2 = jnp.concatenate([g2, jnp.zeros((6, DS), F32)], 0)
-
-    expert_grad, ret = chain(pk, meta, g2, w, C, D)
-    ret = ret.transpose(0, 2, 1, 3).reshape(2, PK, D).astype(F32)
-    out1, back2, back1 = ret[0, :C], ret[0, C:2 * C], ret[1, :C]
-
-    padded = jnp.concatenate([own, ahead], 0)
-    unit_h1, scale_h1 = normed(hidden)
-    unit_e1, _ = normed(padded[1:1 + tokens_here])
-    unit_e2, _ = normed(padded[2:2 + tokens_here])
-    mixed1 = (unit_h1 * norm_gain[0, 0] + unit_e1 * norm_gain[0, 1]).astype(BF16)
-    prev2 = (mixed1.astype(F32) + put_rows(tok[0], out1, weight[0], tokens_here)).astype(BF16)
-    unit_h2, scale_h2 = normed(prev2)
-    dm2 = cot.astype(F32) + put_rows(tok[1], back2, live[1], tokens_here)
-    g2h, g2e = jnp.sum(dm2 * unit_h2, 0), jnp.sum(dm2 * unit_e2, 0)
-    grad1 = norm_back(dm2 * norm_gain[1, 0], unit_h2, scale_h2)
-    dm1 = grad1 + put_rows(tok[0], back1, live[0], tokens_here)
-    g1h, g1e = jnp.sum(dm1 * unit_h1, 0), jnp.sum(dm1 * unit_e1, 0)
-    grad0 = norm_back(dm1 * norm_gain[0, 0], unit_h1, scale_h1)
-    hidden_grad = from_behind(grad0.astype(BF16)[None, None], "section", -1)
-
-    parts = jnp.stack([g1h, g1e, g2h, g2e]).reshape(4, S, DS).transpose(1, 0, 2)
-    parts = jnp.concatenate([parts, jnp.zeros((S, 4, DS), F32)], 1)
-    total = gain_sum(parts)
+    ng = jnp.concatenate([norm_gain.reshape(4, D), jnp.zeros((4, D), F32)], 0)
+    ext = jnp.concatenate([own, ahead, jnp.zeros((PK - 2, D), BF16)], 0)
+    sl = jnp.stack([h_rows, e_rows[:2 * C].astype(BF16), e_rows[2 * C:].astype(BF16), c_rows.astype(BF16)])
+    sl = jnp.pad(sl, ((0, 0), (0, PK - 2 * C), (0, 0)))
+
+    expert_grad, grads, slot_grads, total = chain(pk, meta, slots, g2, w, mh, ext, cot, sl, ng, C)
+    put = pick(back_to, tokens_here)
+    hit = jnp.sum(put.astype(F32), axis=0)
+    placed = lax.dot_general(
+        put, slot_grads[:2 * C], (((0,), (0,)), ((), ())), preferred_element_type=F32
+    )
+    hidden_grad = jnp.where(hit[:, None] > 0.5, placed.astype(BF16), grads)
     Q = lax.axis_size("dp")
     wide = DS // Q
     gain_grad = lax.dynamic_slice(total, (0, lax.axis_index("dp") * wide), (4, wide))
-    return (hidden_grad, expert_grad[None], gain_grad.reshape(1, 2, 2, wide))
+    return (hidden_grad[None, None], expert_grad[None], gain_grad.reshape(1, 2, 2, wide))
 
 
 def solution(mesh):

time: 319 us -> 273 us (0.86)
  other arithmetic: 29.8 us -> 7.17 us
  waiting for transfers between devices: 16.1 us -> 1.07 us
  local copies, waits for them, and re-layouts: 24.4 us -> 15.6 us
  matrix products: 6.58 us -> 10.3 us
  starting transfers between devices: 8.25 us -> 4.67 us
    ppermute x4 -> x2, waiting for transfers between devices: 16.1 us -> 1.06 us  [from_behind(): return lax.ppermute(value, axis, pairs)]
    reduce_sum x2 -> x1, other arithmetic: 10.8 us -> 0.09 us  [local(): hit = jnp.sum(put.astype(F32), axis=0)]
    reduce_sum x6 -> x3, other arithmetic: 8.92 us -> 0.56 us  [normed(): scale = lax.rsqrt(jnp.mean(wide * wide, axis=-1, keepdims=True) + eps_norm)]
    slice x2, local copies, waits for them, and re-layouts: 4.56 us -> 0.67 us  [the longest x1 0.66 us: local(): mixed = (unit_h * norm_gain[0, 0] + unit_e * norm_gain[0, 1]).astype(BF16)]
    dot_general x0 -> x1, matrix products: none -> 3.75 us  [local(): lax.dot_general(put, slot_grads[:2 * C], (((0,), (0,)), ((), ())), prefer...]
    ppermute x4 -> x2, starting transfers between devices: 6.95 us -> 3.37 us  [from_behind(): return lax.ppermute(value, axis, pairs)]
    pallas_call x2 -> x1, Pallas kernels: 230 us -> 231 us  [chain(): pl.pallas_call(functools.partial(chain_kernel, S, Q, X, C, D), out_shape=...]
  transfers between devices with their start and end apart: 5 -> 3, of which waited for: 1 -> 1; matrix products, arithmetic and copies ran while one was open for 11% -> 7% of each run, Pallas kernels for 73% -> 0%
where the time goes in v2:
time: 273 us; the launch traced here: 270 us
  Pallas kernels  231 us (85%)
  local copies, waits for them, and re-layouts  15.6 us (6%)
  matrix products  10.3 us (4%)
  other arithmetic  7.17 us (3%)
  starting transfers between devices  4.67 us (2%)
    pallas_call x1, Pallas kernels, chain(): pl.pallas_call(functools.partial(chain_kernel, S, Q, X, C, D), out_shape=...  231 us
    dot_general x4, matrix products, dot_nn(): lax.dot_general(a, b, (((1,), (0,)), ((), ())), preferred_element_type=F32)  6.52 us
  transfers between devices with their start and end apart: 3, of which 1 were waited for; matrix products, arithmetic and copies ran while one was open for 7% of the time, Pallas kernels for 0%

profile of v2, /device:TPU:1, one launch (start us, length us, event | category | flops | bytes accessed | tf_op | source)
XLA Modules:
  0.0 270.3 jit_solution(10401286348566034302)
XLA Ops:
  0.7 0.8 slice_bitcast_fusion.6
  1.5 0.8 stack_reshape_squeeze.3
  2.3 0.7 iota_compare_fusion.10
  3.0 0.2 select_multiply_fusion
  3.2 0.1 reshape.162
  3.3 3.4 %collective-permute-start = (s32[2,12]{1,0:T(2,128)S(1)}, s32[2,12]{1,0:T(2,128)S(1)}, u32[]{:S(2)}, u32[]{:S(2)}) collective-permute-start(s32[2,12]{1,0:T(2,128)S(1)} %pad_add_fusion), channel_id=1, source_target_pairs={{0,192},{64,0},{128,64},{192,128},{1,193},{65,1},{129,65},{193,129... | collective-permute-start | bytes 296 | tf_op jit(solution)/shard_map/ppermute | solution.py:20
  6.7 0.9 slice_bitcast_fusion
  7.6 1.3 collective-permute-start.2
  8.9 0.8 reshape_squeeze.3
  9.7 0.6 bitcast_convert_fusion
  10.3 2.7 fusion.33
  13.0 0.6 copy-done.2
  13.8 0.7 fusion.30
  14.5 0.1 reshape.163
  14.7 0.4 fusion.18
  15.1 0.6 slice_bitcast_fusion.1
  15.7 0.1 lt.39
  15.8 0.6 mul.138
  16.3 0.7 pad.36.clone
  17.0 0.7 pad.23.clone
  17.7 0.6 concatenate.26.g2
  18.3 0.7 concatenate.28.ng
  19.1 0.6 select_maximum_fusion.slots
  19.7 2.6 convolution_convert_fusion.1
  22.3 0.1 convert_reduce_fusion
  22.4 0.5 broadcast_compare_fusion
  22.9 0.9 convolution_add_fusion
  23.9 0.2 multiply_reduce_fusion
  24.0 0.8 fusion.13
  24.9 0.2 multiply_reduce_fusion.1
  25.1 0.1 pad_maximum_fusion
  25.2 0.3 stack.39
  25.5 0.9 copy.14
  26.5 0.6 pad.14.meta
  27.1 1.8 maximum_maximum_fusion.ext
  28.9 1.1 collective-permute-done.1
  29.9 0.2 fusion.9
  30.2 0.2 fusion.12
  30.3 0.1 slice_multiply_fusion.1
  30.4 0.1 maximum_maximum_fusion.1
  30.6 0.3 stack.38
  30.9 0.2 copy.13
  31.1 0.8 maximum_bitcast_fusion.pk
  31.9 1.1 fusion.8.sl
  33.0 230.7 %expert_chain.1 = (bf16[2,3,448,512]{3,2,1,0:T(8,128)(2,1)}, bf16[128,7168]{1,0:T(8,128)(2,1)}, bf16[16,7168]{1,0:T(8,128)(2,1)}, f32[4,448]{1,0:T(4,128)}) custom-call(bf16[2,16,16,448]{3,2,1,0:T(8,128)(2,1)} %maximum_bitcast_fusion.pk, f32[8,128]{1,0:T(8,128)} %pad.14.meta, f32[8,128]{1,0:T(8,128)} %select_maximum_fusion.slots, f32[8,448]{1,0:T(8,128)} %concatenate.26.g2, ...), custom_call_target="tpu_custom_call" | custom-call | tf_op jit(solution)/shard_map/expert_chain/pallas_call | solution.py:589
  263.7 1.3 constant_dynamic-slice_fusion
  265.1 3.7 %fusion.1 = bf16[1,1,128,7168]{3,2,1,0:T(8,128)(2,1)} fusion(bf16[128,7168]{1,0:T(8,128)(2,1)} %get-tuple-element.8, pred[128]{0:T(512)(128)(4,1)S(1)} %copy-done.22, bf16[16,7168]{1,0:T(8,128)(2,1)} %get-tuple-element.7, s32[12]{0:T(128)S(1)} %copy-done.15), kind=kOutput, calls=%fused_computation.2 | convolution fusion | flops 23856640 | bytes 3899568 | tf_op jit(solution)/shard_map/dot_general | solution.py:702
  268.8 1.5 copy.16
  (77 shorter events, 0.7 us)
Async XLA Ops:
  0.6 13.0 %copy-start.17 = (s32[1,1,2,1]{2,3,1,0:T(1,128)S(1)}, s32[1,1,2,1]{2,3,1,0:T(1,128)}, u32[]{:S(2)}) copy-start(s32[1,1,2,1]{2,3,1,0:T(1,128)} %param.12) | copy-start | bytes 28
  0.6 14.1 %copy-start = (bf16[1,1,128,7168]{3,2,1,0:T(8,128)(2,1)S(1)}, bf16[1,1,128,7168]{3,2,1,0:T(8,128)(2,1)}, u32[]{:S(2)}) copy-start(bf16[1,1,128,7168]{3,2,1,0:T(8,128)(2,1)} %param.9) | copy-start | bytes 5505028
  0.7 13.0 %copy-start.20 = (f32[1,1,2,6]{3,2,1,0:T(2,128)S(1)}, f32[1,1,2,6]{3,2,1,0:T(2,128)}, u32[]{:S(2)}) copy-start(f32[1,1,2,6]{3,2,1,0:T(2,128)} %param.13) | copy-start | bytes 148
  0.7 13.2 %copy-start.8 = (f32[2,2,7168]{2,1,0:T(2,128)S(1)}, f32[2,2,7168]{2,1,0:T(2,128)}, u32[]{:S(2)}) copy-start(f32[2,2,7168]{2,1,0:T(2,128)} %param.14) | copy-start | bytes 344068
  3.0 7.3 %copy-start.12 = (f32[6]{0:T(128)}, f32[6]{0:T(128)S(1)}, u32[]{:S(2)}) copy-start(f32[6]{0:T(128)S(1)} %get-tuple-element.27) | copy-start | bytes 76
  3.3 16.4 %collective-permute-start = (s32[2,12]{1,0:T(2,128)S(1)}, s32[2,12]{1,0:T(2,128)S(1)}, u32[]{:S(2)}, u32[]{:S(2)}) collective-permute-start(s32[2,12]{1,0:T(2,128)S(1)} %pad_add_fusion), channel_id=1, source_target_pairs={{0,192},{64,0},{128,64},{192,128},{1,193},{65,1},{129,65},{193,129... | collective-permute-start | bytes 296 | tf_op jit(solution)/shard_map/ppermute | solution.py:20
  7.6 15.3 %collective-permute-start.2 = (bf16[2,7168]{1,0:T(2,128)(2,1)S(1)}, bf16[2,7168]{1,0:T(2,128)(2,1)S(1)}, u32[]{:S(2)}, u32[]{:S(2)}) collective-permute-start(bf16[2,7168]{1,0:T(2,128)(2,1)S(1)} %slice_bitcast_fusion), channel_id=1, source_target_pairs={{4,0},{8,4},{12,8},{16,12},{20,16},{24,20},{28,24},{32,28},{36,32}... | collective-permute-start | bytes 86024 | tf_op jit(solution)/shard_map/ppermute | solution.py:26
  12.9 0.7 copy-start.2
  12.9 4.7 %slice-start = ((f32[2,2,7168]{2,1,0:T(2,128)}), f32[1,2,7168]{2,1,0:T(2,128)S(1)}, s32[]{:S(2)}) async-start(f32[2,2,7168]{2,1,0:T(2,128)} %param.14), calls=%async_computation | async-start | bytes 114688 | tf_op jit(solution)/shard_map/slice | solution.py:692
  14.7 4.9 %copy-start.11 = (pred[24,130]{1,0:T(8,128)(4,1)}, pred[24,130]{1,0:T(8,128)(4,1)S(1)}, u32[]{:S(2)}) copy-start(pred[24,130]{1,0:T(8,128)(4,1)S(1)} %iota_compare_fusion.1) | copy-start | bytes 9364
  19.7 3.2 %copy-start.14 = (s32[12]{0:T(128)}, s32[12]{0:T(128)S(1)}, u32[]{:S(2)}) copy-start(s32[12]{0:T(128)S(1)} %get-tuple-element.21) | copy-start | bytes 148
  22.3 2.6 copy-start.5
  22.3 2.6 copy-start.13
  22.3 2.6 copy-start.16
  22.3 7.6 %collective-permute-start.1 = (bf16[12,7168]{1,0:T(8,128)(2,1)}, bf16[12,7168]{1,0:T(8,128)(2,1)S(1)}, u32[]{:S(2)}, u32[]{:S(2)}) collective-permute-start(bf16[12,7168]{1,0:T(8,128)(2,1)} %convolution_convert_fusion.1), channel_id=1, source_target_pairs={{0,64},{64,128},{128,192},{192,0},{1,65},{65,129},{129,193},{193,1... | collective-permute-start | bytes 516104 | tf_op jit(solution)/shard_map/ppermute | solution.py:20
  23.8 2.6 copy-start.18
  23.8 2.5 copy-start.19
  23.8 3.2 %copy-start.23 = (bf16[144]{0:T(256)(128)(2,1)S(1)}, bf16[144]{0:T(256)(128)(2,1)}, u32[]{:S(2)}) copy-start(bf16[144]{0:T(256)(128)(2,1)} %pad.23.clone) | copy-start | bytes 868
  27.1 3.0 %copy-start.9 = (f32[1,1,7168]{2,1,0:T(1,128)S(1)}, f32[1,1,7168]{2,1,0:T(1,128)}, u32[]{:S(2)}) copy-start(f32[1,1,7168]{2,1,0:T(1,128)} %get-tuple-element.17) | copy-start | bytes 86020
  27.1 3.0 %copy-start.10 = (f32[1,1,7168]{2,1,0:T(1,128)S(1)}, f32[1,1,7168]{2,1,0:T(1,128)}, u32[]{:S(2)}) copy-start(f32[1,1,7168]{2,1,0:T(1,128)} %get-tuple-element.18) | copy-start | bytes 86020
  27.1 3.3 %copy-start.24 = (bf16[6]{0:T(256)(128)(2,1)S(1)}, bf16[6]{0:T(256)(128)(2,1)}, u32[]{:S(2)}) copy-start(bf16[6]{0:T(256)(128)(2,1)} %bitcast_convert_fusion) | copy-start | bytes 40
  27.1 3.3 %copy-start.21 = (bf16[16]{0:T(256)(128)(2,1)S(1)}, bf16[16]{0:T(256)(128)(2,1)}, u32[]{:S(2)}) copy-start(bf16[16]{0:T(256)(128)(2,1)} %pad.36.clone) | copy-start | bytes 100
  28.9 2.2 copy-start.4
  30.1 1.8 copy-start.3
  30.1 1.8 copy-start.6
  30.2 1.8 copy-start.7
  33.0 232.0 %copy-start.15 = (s32[12]{0:T(128)S(1)}, s32[12]{0:T(128)}, u32[]{:S(2)}) copy-start(s32[12]{0:T(128)} %copy-done.14) | copy-start | bytes 148
  33.0 232.0 %copy-start.22 = (pred[128]{0:T(512)(128)(4,1)S(1)}, pred[128]{0:T(512)(128)(4,1)}, u32[]{:S(2)}) copy-start(pred[128]{0:T(512)(128)(4,1)} %broadcast_compare_fusion) | copy-start | bytes 388
  265.1 3.8 %copy-start.1 = (bf16[2,3,448,512]{3,2,1,0:T(8,128)(2,1)S(1)}, bf16[2,3,448,512]{3,2,1,0:T(8,128)(2,1)}, u32[]{:S(2)}) copy-start(bf16[2,3,448,512]{3,2,1,0:T(8,128)(2,1)} %get-tuple-element.9) | copy-start | bytes 8257540

commit v3 on v2

--- a/solution.py
+++ b/solution.py
@@ -112,12 +112,13 @@
     for to in sections:
         pl.semaphore_signal(barrier, inc=1, device_id={"section": to}, device_id_type=MESH)
         total += 1
-    pl.semaphore_wait(barrier, total)
-
-
-def chain_kernel(S, Q, X, C, D, pk, meta, slots, g2, w, mh, ext, cot, sl, ng, eg, hg, slr, gains,
-                 ret, land, mland, rows, xr, do, gu, lg, da, ld, act, dg, op, lo, pv, ss, ssl, od, rb, gsv,
-                 hid, hgs, es, mx, dmx, ad, sls, gacc, gsrc, gland, gown, gland2, send, recv, xsend, xrecv):
+    return lambda: pl.semaphore_wait(barrier, total)
+
+
+def chain_kernel(S, Q, X, C, D, slots, g2, w, mh, own, ahead, cot, ng, eg, hg, slr, gains, asks,
+                 ext, hsend, hrow, se, sc, pka, pkb, landa, landb, meta, mland, rows, ret, rb, xr, do, gu, lg, da,
+                 ld, act, dg, op, lo, pv, ss, ssl, od, gsv, hid, hgs, es, mx, dmx, ad, sls, gacc, gsrc, gland,
+                 gown, gland2, send, recv, xsend, xrecv):
     me = lax.axis_index("seq")
     d = lax.axis_index("dp")
     sec = lax.axis_index("section")
@@ -149,9 +150,10 @@
     def dp_wait(ph, dst_of):
         wires.wait(ph, "dp", Q, d, dst_of)
 
-    greet((("seq", S, me), ("dp", Q, d)), (after, before_me))
-
+    barrier_axes = (("seq", S, me), ("dp", Q, d))
+    greet_all = greet(barrier_axes, (after, before_me))
     NC = mh.shape[0] // PK
+    T = mh.shape[0]
 
     def chunk(c):
         return pl.ds(pl.multiple_of(c * PK, PK), PK)
@@ -168,6 +170,9 @@
     def hg_copy(c):
         return hop(hgs.at[chunk(c), :], hg.at[chunk(c), :], NC + c, before_me)
 
+    ask_hop = hop(slots, asks, 2 * NC + 1, before_me)
+    row_hop = hop(hsend, hrow, 2 * NC + 2, after)
+
     def each_chunk(fn, first=0, last=NC):
         def body(c, carry):
             fn(c)
@@ -175,23 +180,59 @@
 
         lax.fori_loop(first, last, body, 0)
 
+    slot_row, live_row, weight_row, fresh_row = (slots[k:k + 1, :] for k in range(4))
+    lane16 = lax.broadcasted_iota(jnp.int32, (PK, 128), 1)
+    line16 = lax.broadcasted_iota(jnp.int32, (PK, 128), 0)
+    line1 = lax.broadcasted_iota(jnp.int32, (PK, 1), 0)
+
+    def column(row):
+        return jnp.sum(jnp.where(lane16 == line16, row, 0.0), axis=1, keepdims=True)
+
+    def line(col, first):
+        return jnp.sum(jnp.where((lane16 == line16 + first) & (line16 < C), col, 0.0), axis=0, keepdims=True)
+
+    slot_tok, slot_live, slot_w = column(slot_row), column(live_row), column(weight_row)
+
+    ext[0:T, :] = own[...]
+    ext[T:T + PK, :] = ahead[...]
+    wide = lax.broadcasted_iota(jnp.int32, (PK, T + PK), 1).astype(F32)
+    for k in range(2):
+        se[k] = dot_nn(jnp.where(wide == slot_tok + (k + 1.0), 1.0, 0.0).astype(BF16), ext[...]).astype(BF16)
+    sc[...] = dot_nn(jnp.where(lane16.astype(F32) == slot_tok, 1.0, 0.0).astype(BF16), cot[...]).astype(BF16)
+
+    greet_all()
+    ask_hop.start()
+
+    first_rows = line1 < C
+
+    def dslice(b):
+        return slice(b * DS, (b + 1) * DS)
+
+    cot_w = jnp.where(first_rows, 1.0, slot_w)
+    for b in range(S):
+        pka[0, b] = (sc[:, dslice(b)].astype(F32) * cot_w).astype(BF16)
+    ph_a = seq_start(lambda to: pka.at[0, to], landa.at[0, me])
+    landa[0, me] = pka[0, me]
+    e_live = jnp.where(first_rows, 1.0, slot_live)
+    for b in range(S):
+        both = jnp.where(first_rows, se[0, :, dslice(b)].astype(F32), se[1, :, dslice(b)].astype(F32))
+        pka[1, b] = (both * e_live).astype(BF16)
+
+    ask_hop.wait_recv()
+    asked = jnp.sum(jnp.where(lane16 == line16, asks[0:1, :], 0.0), axis=1, keepdims=True)
+    hsend[...] = dot_nn(jnp.where(lane16.astype(F32) == asked, 1.0, 0.0).astype(BF16), mh[...]).astype(BF16)
+    row_hop.start()
     each_chunk(lambda c: hid_copy(c).start())
-
-    def blk(b):
-        return pl.ds(pl.multiple_of(b * PK, PK), PK)
-
-    ph_b = seq_start(lambda to: pk.at[0, to], land.at[0, blk(me), :])
-    ph_m = seq_start(lambda to: meta, mland.at[me])
-    ph_a = seq_start(lambda to: pk.at[1, to], land.at[1, blk(me), :])
-    land[0, blk(me), :] = pk[0, me]
-    land[1, blk(me), :] = pk[1, me]
-    mland[me] = meta[...]
-
-    def unpack(k):
-        r = lax.broadcasted_iota(jnp.int32, (S * PK, S * PK), 0)
-        c = lax.broadcasted_iota(jnp.int32, (S * PK, S * PK), 1)
-        perm = jnp.where(c == (r % S) * PK + r // S, 1.0, 0.0).astype(BF16)
-        rows[k] = dot_nn(perm, land[k])
+    ph_e = seq_start(lambda to: pka.at[1, to], landa.at[1, me])
+    landa[1, me] = pka[1, me]
+
+    def unpack(k, land, height, first):
+        n = S * height
+        r = lax.broadcasted_iota(jnp.int32, (n, n), 0)
+        c = lax.broadcasted_iota(jnp.int32, (n, n), 1)
+        perm = jnp.where(c == (r % S) * height + r // S, 1.0, 0.0).astype(BF16)
+        flat = land[...].astype(F32).reshape(n, DS).astype(BF16)
+        rows[k, first * S:(first + height) * S, :] = dot_nn(perm, flat)
 
     def rows_at(k, slot):
         return rows[k, slot * S:(slot + 1) * S, :]
@@ -352,8 +393,9 @@
             if dm1_add is not None:
                 dm1 = dm1 + dm1_add(at)
             n1 = h_at(at) * sh
-            collect(0, at, dm1 * n1, mask)
-            collect(1, at, dm1 * (e_at(0, at) * se1), mask)
+            if mask is not None:
+                collect(0, at, dm1 * n1, mask)
+                collect(1, at, dm1 * (e_at(0, at) * se1), mask)
             u = dm1 * gain(0, at)
             dmx[:, at] = u
             return (acc[0] + u * n1,)
@@ -365,13 +407,6 @@
             return acc
 
         sweep(last, 0)
-
-    slot_row, live_row, weight_row, fresh_row = (slots[k:k + 1, :] for k in range(4))
-    lane16 = lax.broadcasted_iota(jnp.int32, (PK, 128), 1)
-    line16 = lax.broadcasted_iota(jnp.int32, (PK, 128), 0)
-
-    def column(row):
-        return jnp.sum(jnp.where(lane16 == line16, row, 0.0), axis=1, keepdims=True)
 
     def bulk_chunk(c):
         hid_copy(c).wait_recv()
@@ -403,36 +438,80 @@
     gacc[...] = jnp.zeros_like(gacc)
 
     def slot_h(at):
-        return sl[0, :, at].astype(F32)
+        return hrow[:, at].astype(F32)
 
     def slot_e(k, at):
-        return sl[1 + k, :, at].astype(F32)
+        return se[k, :, at].astype(F32)
 
     slot_mask = column(fresh_row)
-    slot_tok = column(slot_row)
     same_tok = jnp.where(slot_tok == slot_row, live_row, 0.0)
     prev_sel = jnp.where(lane16 < C, same_tok, 0.0)
     prev_w = jnp.sum(prev_sel * weight_row, axis=1, keepdims=True)
-    dm2_sel = jnp.where((lane16 >= C) & (lane16 < 2 * C), same_tok, 0.0)
+    dm2_tok = jnp.where(slot_tok == slots[5:6, :], slots[6:7, :], 0.0)
+    dm2_sel = jnp.where(lane16 < C, dm2_tok, 0.0)
 
     def widen(n, sel, k, scale_by):
         for b in range(S):
-            part = dot_nn(sel[:, :PK].astype(BF16), ret[k, b])
+            part = dot_nn(sel[:, :8].astype(BF16), ret[k, b])
             if scale_by is not None:
                 part = part * scale_by
-            ad[n, :, b * DS:(b + 1) * DS] = part
-
-    seq_wait(ph_b, lambda frm: land.at[0, blk(frm), :])
-    unpack(0)
-    xr[0, rowslice(d), :] = rows[0, 0:RW, :].astype(BF16)
+            ad[n, :, dslice(b)] = part
+
+    def send_back(k):
+        r = lax.broadcasted_iota(jnp.int32, (S * 8, RW), 0)
+        c = lax.broadcasted_iota(jnp.int32, (S * 8, RW), 1)
+        perm = jnp.where(c == (r % 8) * S + r // 8, 1.0, 0.0).astype(BF16)
+        rb[k] = dot_nn(perm, od[k * RW:(k + 1) * RW, :]).reshape(S, 8, DS).astype(BF16)
+        ph = seq_start(lambda to: rb.at[k, to], ret.at[k, me])
+        ret[k, me] = rb[k, me]
+        return ph
+
+    seq_wait(ph_a, lambda frm: landa.at[0, frm])
+    unpack(0, landa.at[0], PK, 0)
+    do[1, rowslice(d), :] = rows[0, RW:2 * RW, :].astype(BF16)
+    ph_d2 = gather_dp(1, do)
+
+    row_hop.wait_recv()
+
+    def slot_squares(at, acc):
+        h, e1, e2 = slot_h(at), slot_e(0, at), slot_e(1, at)
+        return acc[0] + h * h, acc[1] + e1 * e1, acc[2] + e2 * e2
+
+    sh, se1, se2 = [lax.rsqrt(v + eps_norm) for v in sweep(slot_squares, 3)]
+
+    def slot_mix(at, acc):
+        m = (slot_h(at) * sh) * gain(0, at) + (slot_e(0, at) * se1) * gain(1, at)
+        mx[:, at] = m.astype(BF16).astype(F32) * slot_live
+        return acc
+
+    sweep(slot_mix, 0)
+    for b in range(S):
+        part = mx[:, dslice(b)]
+        pkb[0, b] = part[:8].astype(BF16)
+        pkb[1, b] = part[8:].astype(BF16)
+        pkb[2, b] = hrow[:, dslice(b)].astype(F32)[:8].astype(BF16)
+    ph_b = seq_start(lambda to: pkb.at[0, to], landb.at[0, me])
+    se2_t2 = pltpu.roll(jnp.broadcast_to(se2, (PK, 128)), PK - C, 0)
+    top = slots[4:5, :] + line(se2_t2, 8) + line(sh, 52) + line(se1, 58)
+    meta[...] = jnp.broadcast_to(top, (8, 128)) * jnp.where(line16[:8] == 0, 1.0, 0.0)
+    ph_m = seq_start(lambda to: meta, mland.at[me])
+    mland[me] = meta[...]
+    ph_b1 = seq_start(lambda to: pkb.at[1, to], landb.at[1, me])
+    ph_b2 = seq_start(lambda to: pkb.at[2, to], landb.at[2, me])
+    for k in range(3):
+        landb[k, me] = pkb[k, me]
+    gather_dp_wait(ph_d2, 1, do)
+    seq_wait(ph_b, lambda frm: landb.at[0, frm])
+    unpack(1, landb.at[0], 8, 0)
+    xr[0, rowslice(d), :] = rows[1, 0:RW, :].astype(BF16)
     ph_x = gather_dp(0, xr)
-    seq_wait(ph_a, lambda frm: land.at[1, blk(frm), :])
-    unpack(1)
-    do[1, rowslice(d), :] = rows[1, C * S:2 * C * S, :].astype(BF16)
-    ph_d2 = gather_dp(1, do)
+    ph_da2 = dact(1)
+    seq_wait(ph_b1, lambda frm: landb.at[1, frm])
+    unpack(1, landb.at[1], 8, 8)
+    seq_wait(ph_e, lambda frm: landa.at[1, frm])
+    unpack(2, landa.at[1], PK, 0)
     gather_dp_wait(ph_x, 0, xr)
     ph = gate_up(0)
-    gather_dp_wait(ph_d2, 1, do)
     gsv[0] = gate_up_wait(ph, 0)
     act_piece(0)
     ph = spread_piece(act.at[0])
@@ -443,7 +522,6 @@
         part = dot_nt(act[0, q, 0], w[0, 2, :, q * PC:(q + 1) * PC])
         out = part if out is None else out + part
     ph = reduce_dp(0, out)
-    ph_da2 = dact(1)
     bulk(3 * NC // 8, NC // 2)
     seq_wait(ph_m, lambda frm: mland.at[frm])
     facts = jnp.sum(mland[...], axis=1)
@@ -458,12 +536,12 @@
     od[0:RW, :] = out.astype(BF16)
     cols = []
     for i in range(C):
-        before = rows_at(0, i) + fact(i) * out[i * S:(i + 1) * S]
+        before = rows_at(1, i) + fact(i) * out[i * S:(i + 1) * S]
         before = before.astype(BF16).astype(F32)
         pv[i * S:(i + 1) * S, :] = before
         cols.append(jnp.sum(before * before, axis=1, keepdims=True))
     for j in range(C):
-        before = rows_at(0, C + j)
+        before = rows_at(1, C + j)
         for i in range(C):
             before = before + (ov(j, i) * fact(i)) * out[i * S:(i + 1) * S]
         before = before.astype(BF16).astype(F32)
@@ -475,10 +553,11 @@
 
     for j in range(C):
         unit = pv[(C + j) * S:(C + j + 1) * S, :] * scale[:, C + j:C + j + 1]
-        mixed = unit * gain_h + (rows_at(1, j) * fact(8 + j)) * gain_e
-        od[RW + j * S:RW + (j + 1) * S, :] = mixed.astype(BF16)
-    xr[1, rowslice(d), :] = od[RW:2 * RW, :]
+        mixed = unit * gain_h + (rows_at(2, C + j) * fact(8 + j)) * gain_e
+        od[3 * RW + j * S:3 * RW + (j + 1) * S, :] = mixed.astype(BF16)
+    xr[1, rowslice(d), :] = od[3 * RW:4 * RW, :]
     ph = gather_dp(1, xr)
+    ph_r0 = send_back(0)
     gather_dp_wait(ph, 1, xr)
     ph = gate_up(1)
     bulk(NC // 2, NC)
@@ -495,74 +574,87 @@
     od[RW:2 * RW, :] = back.astype(BF16)
     cols, keep_u, keep_n = [], [], []
     for i in range(C):
-        cot = rows_at(1, 2 * C + i) if i < PK - 2 * C else rows_at(0, 2 * C + i - (PK - 2 * C))
+        top = rows_at(0, i)
         for j in range(C):
-            cot = cot + ov(j, i) * back[j * S:(j + 1) * S]
-        u = cot * gain_h
+            top = top + ov(j, i) * back[j * S:(j + 1) * S]
+        u = top * gain_h
         unit = pv[i * S:(i + 1) * S, :] * scale[:, i:i + 1]
         keep_u.append(u)
         keep_n.append(unit)
         cols.append(jnp.sum(u * unit, axis=1, keepdims=True))
     ph = sums_start(1, cols)
 
-    def send_back(k, lo_row, hi_row):
-        r = lax.broadcasted_iota(jnp.int32, (S * PK, hi_row - lo_row), 0)
-        c = lax.broadcasted_iota(jnp.int32, (S * PK, hi_row - lo_row), 1)
-        perm = jnp.where(c == (r % PK) * S + r // PK, 1.0, 0.0).astype(BF16)
-        rb[k] = dot_nn(perm, od[lo_row:hi_row, :]).astype(BF16)
-        ph = seq_start(lambda to: rb.at[k, blk(to), :], ret.at[k, me])
-        ret[k, me] = rb[k, blk(me), :]
-        return ph
-
     inner = sums_wait(ph, 1)
 
     for i in range(C):
         back = (keep_u[i] - keep_n[i] * inner[:, i:i + 1]) * scale[:, i:i + 1]
-        rows[1, i * S:(i + 1) * S, :] = back * fact(i)
-    do[0, rowslice(d), :] = rows[1, 0:RW, :].astype(BF16)
+        od[3 * RW + i * S:3 * RW + (i + 1) * S, :] = (back * fact(i)).astype(BF16)
+    do[0, rowslice(d), :] = od[3 * RW:4 * RW, :]
     ph = gather_dp(0, do)
+    ph_r1 = send_back(1)
     gather_dp_wait(ph, 0, do)
     ph = dact(0)
     spread_wait(ph_a2, act.at[1])
-    down_grad(1)
-    down_grad(0)
+    seq_wait(ph_r0, lambda frm: ret.at[0, frm])
+    seq_wait(ph_r1, lambda frm: ret.at[1, frm])
+    widen(0, prev_sel, 0, prev_w)
+    widen(1, dm2_sel, 1, None)
+    slot_sh, slot_se1 = rows_pass_1(
+        slot_h, slot_e, lambda at: sc[:, at].astype(F32), slot_mask, lambda at: ad[0, :, at], lambda at: ad[1, :, at]
+    )
+
+    def early(at, acc):
+        collect(0, at, dmx[:, at] * (slot_h(at) * slot_sh), slot_mask)
+        collect(1, at, dmx[:, at] * (slot_e(0, at) * slot_se1), slot_mask)
+        return acc
+
+    sweep(early, 0)
     d_act = dact_wait(ph, 0)
     pre_grads(0, d_act)
     ph = spread_piece(dg.at[0])
-    ph_r0 = send_back(0, 0, 2 * RW)
-    seq_wait(ph_r0, lambda frm: ret.at[0, frm])
-    widen(0, prev_sel, 0, prev_w)
-    widen(1, dm2_sel, 0, None)
-    slot_sh, slot_se1 = rows_pass_1(
-        slot_h, slot_e, lambda at: sl[3, :, at].astype(F32), slot_mask, lambda at: ad[0, :, at], lambda at: ad[1, :, at]
-    )
+    down_grad(1)
+    down_grad(0)
     spread_wait(ph, dg.at[0])
+    for b in range(S):
+        gsrc[b] = jnp.sum(gacc[:, :, dslice(b)], axis=1)
+    ph_g = seq_start(lambda to: gsrc.at[to], gland.at[me])
+    gland[me] = gsrc[me]
     ph = reduce_dp(2, drows(0))
     in_grads(0)
     back = reduce_dp_wait(ph, 2)
     od[2 * RW:3 * RW, :] = back.astype(BF16)
-    ph_r1 = send_back(1, 2 * RW, 3 * RW)
-    seq_wait(ph_r1, lambda frm: ret.at[1, frm])
-    widen(2, prev_sel, 1, None)
+    ph_r2 = send_back(2)
+
+    seq_wait(ph_b2, lambda frm: landb.at[2, frm])
+    unpack(1, landb.at[2], 8, 0)
+    late_h = jnp.zeros((S, DS), F32)
+    late_e = jnp.zeros((S, DS), F32)
+    for i in range(C):
+        part = back[i * S:(i + 1) * S]
+        late_h = late_h + part * (rows_at(1, i) * fact(52 + i))
+        late_e = late_e + part * (rows_at(2, i) * fact(58 + i))
+    seq_wait(ph_g, lambda frm: gland.at[frm])
+    value = add_up(gland)
+    late = jnp.concatenate(
+        [jnp.sum(late_h, axis=0, keepdims=True), jnp.sum(late_e, axis=0, keepdims=True), jnp.zeros((2, DS), F32)], 0
+    )
+    value = value + late
+    QS = DS // Q
+    for q in range(Q):
+        gown[q] = value[:, q * QS:(q + 1) * QS]
+    ph_q = dp_start(lambda to: gown.at[to], gland2.at[d])
+    gland2[d] = gown[d]
+
+    seq_wait(ph_r2, lambda frm: ret.at[2, frm])
+    widen(2, prev_sel, 2, None)
 
     def slot_store(at, value):
         sls[:, at] = value
 
-    rows_pass_2(slot_h, slot_e, slot_mask, slot_sh, slot_se1, lambda at: ad[2, :, at], slot_store)
+    rows_pass_2(slot_h, slot_e, None, slot_sh, slot_se1, lambda at: ad[2, :, at], slot_store)
     back_rows = hop(sls, slr, 2 * NC, before_me)
     back_rows.start()
-
-    for b in range(S):
-        part = gacc[:, :, b * DS:(b + 1) * DS]
-        gsrc[b] = jnp.sum(part, axis=1)
-    ph = seq_start(lambda to: gsrc.at[to], gland.at[me])
-    gland[me] = gsrc[me]
-    seq_wait(ph, lambda frm: gland.at[frm])
-    value = add_up(gland)
-    gown[...] = value
-    ph = dp_start(lambda to: gown, gland2.at[d])
-    gland2[d] = value
-    dp_wait(ph, lambda frm: gland2.at[frm])
+    dp_wait(ph_q, lambda frm: gland2.at[frm])
     gains[...] = add_up(gland2)
 
     def finish(c):
@@ -571,11 +663,13 @@
         hg_copy(c).wait_recv()
 
     each_chunk(finish)
+    ask_hop.wait_send()
+    row_hop.wait_send()
     back_rows.wait()
     wires.drain()
 
 
-def chain(pk, meta, slots, g2, w, mh, ext, cot, sl, ng, C):
+def chain(slots, g2, w, mh, own, ahead, cot, ng, C):
     S, Q, X = lax.axis_size("seq"), lax.axis_size("dp"), lax.axis_size("section")
     DS, HS = w.shape[2], w.shape[3]
     T, D = mh.shape
@@ -585,22 +679,33 @@
     PC = HS // CG
     NC = T // PK
     vm = pltpu.VMEM
-    phases = 24
+    phases = 30
     return pl.pallas_call(
         functools.partial(chain_kernel, S, Q, X, C, D),
         out_shape=(
             jax.ShapeDtypeStruct(w.shape, BF16),
             jax.ShapeDtypeStruct((T, D), BF16),
             jax.ShapeDtypeStruct((PK, D), BF16),
-            jax.ShapeDtypeStruct((4, DS), F32),
+            jax.ShapeDtypeStruct((4, DS // Q), F32),
+            jax.ShapeDtypeStruct((8, 128), F32),
         ),
-        in_specs=[pl.BlockSpec(memory_space=vm)] * 10,
-        out_specs=(pl.BlockSpec(memory_space=vm),) * 4,
+        in_specs=[pl.BlockSpec(memory_space=vm)] * 8,
+        out_specs=(pl.BlockSpec(memory_space=vm),) * 5,
         scratch_shapes=[
+            vm((T + PK, D), BF16),
+            vm((PK, D), BF16),
+            vm((PK, D), BF16),
+            vm((2, PK, D), BF16),
+            vm((PK, D), BF16),
             vm((2, S, PK, DS), BF16),
-            vm((2, S * PK, DS), BF16),
+            vm((3, S, 8, DS), BF16),
+            vm((2, S, PK, DS), BF16),
+            vm((3, S, 8, DS), BF16),
+            vm((8, 128), F32),
             vm((S, 8, 128), F32),
-            vm((2, S * PK, DS), F32),
+            vm((3, S * PK, DS), F32),
+            vm((3, S, 8, DS), BF16),
+            vm((3, S, 8, DS), BF16),
             vm((2, NR, DS), BF16),
             vm((2, NR, DS), BF16),
             vm((2, CG, 2, NR, PC), BF16),
@@ -614,8 +719,7 @@
             vm((2 * RW, DS), F32),
             vm((2, S, 128), F32),
             vm((2, S, S, 128), F32),
-            vm((3 * RW, DS), BF16),
-            vm((2, S * PK, DS), BF16),
+            vm((4 * RW, DS), BF16),
             vm((2, 2, RW, PC), F32),
             vm((T, D), BF16),
             vm((T, D), BF16),
@@ -627,18 +731,18 @@
             vm((4, 8, D), F32),
             vm((S, 4, DS), F32),
             vm((S, 4, DS), F32),
-            vm((4, DS), F32),
-            vm((Q, 4, DS), F32),
+            vm((Q, 4, DS // Q), F32),
+            vm((Q, 4, DS // Q), F32),
             pltpu.SemaphoreType.DMA((phases, S)),
             pltpu.SemaphoreType.DMA((phases, S)),
-            pltpu.SemaphoreType.DMA((2 * NC + 1,)),
-            pltpu.SemaphoreType.DMA((2 * NC + 1,)),
+            pltpu.SemaphoreType.DMA((2 * NC + 3,)),
+            pltpu.SemaphoreType.DMA((2 * NC + 3,)),
         ],
         compiler_params=pltpu.CompilerParams(
             collective_id=0, has_side_effects=True, vmem_limit_bytes=60 * 1024 * 1024
         ),
         name="expert_chain",
-    )(pk, meta, slots, g2, w, mh, ext, cot, sl, ng)
+    )(slots, g2, w, mh, own, ahead, cot, ng)
 
 
 def pick(index, count):
@@ -659,54 +763,35 @@
     same = (tok[1][:, None] == tok[0][None, :]).astype(F32) * live[1][:, None] * live[0][None, :]
     fresh = jnp.stack([live[0], live[1] * (1.0 - jnp.max(same, axis=1))]).reshape(-1)
     flat = tok.reshape(-1)
-    merge = jnp.where(fresh > 0.5, flat, -1)
-
-    asked, back_to = from_behind(jnp.stack([flat, merge]), "section", -1)
-    sent = dot_nn(pick(asked, tokens_here), mh).astype(BF16)
-    h_rows = from_behind(sent, "section", 1)
-
-    places = jnp.concatenate([flat + 1, flat + 2])
-    e_pick = pick(places, tokens_here + 2)
-    e_rows = dot_nn(e_pick[:, :tokens_here], own) + dot_nn(e_pick[:, tokens_here:], ahead)
-    c_rows = dot_nn(pick(flat, tokens_here), cot)
-    unit_h, _ = normed(h_rows)
-    unit_e, _ = normed(e_rows[:2 * C])
-    mixed = (unit_h * norm_gain[0, 0] + unit_e * norm_gain[0, 1]).astype(BF16)
-    e2 = e_rows[3 * C:]
-    _, se2 = normed(e2)
-    m1 = mixed[:C] * live[0][:, None].astype(BF16)
-    e2 = (e2 * live[1][:, None]).astype(BF16)
-    dout2 = (c_rows[C:] * weight[1][:, None]).astype(BF16)
-    c1 = c_rows[:C].astype(BF16)
-    cut = PK - 2 * C
-    pad = jnp.zeros((2 * PK - 5 * C, D), BF16)
-    pk_b = jnp.concatenate([m1, mixed[C:], c1[cut:], pad], 0)
-    pk_a = jnp.concatenate([e2, dout2, c1[:cut]], 0)
-    pk = jnp.stack([pk_b, pk_a]).reshape(2, PK, S, DS).transpose(0, 2, 1, 3)
-    facts = jnp.concatenate(
-        [weight[0], jnp.zeros((8 - C,), F32), se2[:, 0], jnp.zeros((8 - C,), F32), same.reshape(-1)]
-    )
-    meta = jnp.pad(facts[None, :], ((0, 7), (0, 128 - facts.shape[0])))
-    slots = jnp.stack([flat.astype(F32), live.reshape(-1), weight.reshape(-1), fresh])
-    slots = jnp.pad(slots, ((0, 4), (0, 128 - 2 * C)))
+
+    def lanes(*parts):
+        row = jnp.concatenate(parts)
+        return jnp.pad(row, (0, 128 - row.shape[0]))
+
+    slots = jnp.stack([
+        lanes(flat.astype(F32)),
+        lanes(live.reshape(-1)),
+        lanes(weight.reshape(-1)),
+        lanes(fresh),
+        lanes(weight[0], jnp.zeros((16 - C,), F32), same.reshape(-1)),
+        lanes(tok[1].astype(F32)),
+        lanes(live[1]),
+        lanes(flat[:1].astype(F32) * 0.0),
+    ])
     g2 = lax.dynamic_slice(norm_gain[1], (0, me * DS), (2, DS))
     g2 = jnp.concatenate([g2, jnp.zeros((6, DS), F32)], 0)
-    ng = jnp.concatenate([norm_gain.reshape(4, D), jnp.zeros((4, D), F32)], 0)
-    ext = jnp.concatenate([own, ahead, jnp.zeros((PK - 2, D), BF16)], 0)
-    sl = jnp.stack([h_rows, e_rows[:2 * C].astype(BF16), e_rows[2 * C:].astype(BF16), c_rows.astype(BF16)])
-    sl = jnp.pad(sl, ((0, 0), (0, PK - 2 * C), (0, 0)))
-
-    expert_grad, grads, slot_grads, total = chain(pk, meta, slots, g2, w, mh, ext, cot, sl, ng, C)
+    ahead = jnp.pad(ahead, ((0, PK - 2), (0, 0)))
+    ng = norm_gain.reshape(4, D)
+
+    expert_grad, grads, slot_grads, total, asks = chain(slots, g2, w, mh, own, ahead, cot, ng, C)
+    back_to = jnp.where(asks[3, :2 * C] > 0.5, asks[0, :2 * C], -1.0).astype(jnp.int32)
     put = pick(back_to, tokens_here)
     hit = jnp.sum(put.astype(F32), axis=0)
     placed = lax.dot_general(
         put, slot_grads[:2 * C], (((0,), (0,)), ((), ())), preferred_element_type=F32
     )
     hidden_grad = jnp.where(hit[:, None] > 0.5, placed.astype(BF16), grads)
-    Q = lax.axis_size("dp")
-    wide = DS // Q
-    gain_grad = lax.dynamic_slice(total, (0, lax.axis_index("dp") * wide), (4, wide))
-    return (hidden_grad[None, None], expert_grad[None], gain_grad.reshape(1, 2, 2, wide))
+    return (hidden_grad[None, None], expert_grad[None], total.reshape(1, 2, 2, -1))
 
 
 def solution(mesh):

time: 273 us -> 251 us (0.919)
  matrix products: 10.3 us -> 3.75 us
  local copies, waits for them, and re-layouts: 15.6 us -> 9.29 us
  other arithmetic: 7.17 us -> 3.37 us
  starting transfers between devices: 4.67 us -> 1.29 us
    dot_general x4 -> x0, matrix products: 6.52 us -> none  [dot_nn(): lax.dot_general(a, b, (((1,), (0,)), ((), ())), preferred_element_type=F32)]
    ppermute x2 -> x0, starting transfers between devices: 3.37 us -> none  [from_behind(): return lax.ppermute(value, axis, pairs)]
  transfers between devices with their start and end apart: 3 -> 1, of which waited for: 1 -> 0; matrix products, arithmetic and copies ran while one was open for 7% -> 3% of each run, Pallas kernels for 0% -> 0%
where the time goes in v3:
time: 251 us
  Pallas kernels  232 us (92%)
  local copies, waits for them, and re-layouts  9.29 us (4%)
  matrix products  3.75 us (1%)
  other arithmetic  3.37 us (1%)
    pallas_call x1, Pallas kernels, chain(): pl.pallas_call(functools.partial(chain_kernel, S, Q, X, C, D), out_shape=...  232 us
  transfers between devices with their start and end apart: 1, of which 0 were waited for; matrix products, arithmetic and copies ran while one was open for 3% of the time, Pallas kernels for 0%

profile of v3, /device:TPU:1, one launch (start us, length us, event | category | flops | bytes accessed | tf_op | source)
XLA Modules:
  0.0 250.7 jit_solution(14337600098396419351)
XLA Ops:
  0.6 0.9 slice_bitcast_fusion
  1.6 1.3 collective-permute-start
  2.9 0.8 reshape_squeeze.3
  3.6 0.8 fusion.10
  4.4 0.8 squeeze.12
  5.1 0.8 bitcast_select_fusion
  5.9 0.7 fusion.11
  6.7 0.1 lt.27
  6.8 0.2 select_multiply_fusion
  7.0 0.1 mul.48
  7.1 0.1 reshape.71
  7.2 0.8 slice.48
  8.0 0.1 dynamic-slice_bitcast_fusion
  8.1 0.1 fusion.8
  8.1 1.6 reshape.72.ng
  9.8 0.6 concatenate.7.g2
  10.4 0.6 stack.44.slots
  11.0 0.0 collective-permute-done
  11.0 0.7 pad.42.ahead
  11.7 232.2 %expert_chain.1 = (bf16[2,3,448,512]{3,2,1,0:T(8,128)(2,1)}, bf16[128,7168]{1,0:T(8,128)(2,1)}, bf16[16,7168]{1,0:T(8,128)(2,1)}, f32[4,112]{1,0:T(4,128)}, f32[8,128]{1,0:T(8,128)}) custom-call(f32[8,128]{1,0:T(8,128)} %stack.44.slots, f32[8,448]{1,0:T(8,128)} %concatenate.7.g2, bf16[2,3,448,512]{3,2,1,0:T(8,128)(2,1)} %w.1, bf16[128,7168]{1,0:T(8,128)(2,1)} %bitcast.49, ...), custom_call_target="tpu_custom_call" | custom-call | tf_op jit(solution)/shard_map/expert_chain/pallas_call | solution.py:683
  243.9 0.7 fusion.7
  244.7 0.1 convert_reduce_fusion
  244.8 0.0 copy-start
  244.8 3.7 %fusion.1 = bf16[1,1,128,7168]{3,2,1,0:T(8,128)(2,1)} fusion(bf16[128,7168]{1,0:T(8,128)(2,1)} %get-tuple-element.10, pred[128]{0:T(512)(128)(4,1)S(1)} %broadcast_compare_fusion, bf16[16,7168]{1,0:T(8,128)(2,1)} %get-tuple-element.9, s32[12]{0:T(128)S(1)} %fusion.7), kind=kOutput, calls=%fused_computation.2 | convolution fusion | flops 23856640 | bytes 3899568 | tf_op jit(solution)/shard_map/dot_general | solution.py:790
  248.5 0.0 copy-done
  248.5 0.0 copy-start.1
  248.5 1.5 copy.13
  250.1 0.0 copy-done.1
  250.1 0.6 copy.14
  (12 shorter events, 0.1 us)
Async XLA Ops:
  1.6 9.5 %collective-permute-start = (bf16[2,7168]{1,0:T(2,128)(2,1)S(1)}, bf16[2,7168]{1,0:T(2,128)(2,1)S(1)}, u32[]{:S(2)}, u32[]{:S(2)}) collective-permute-start(bf16[2,7168]{1,0:T(2,128)(2,1)S(1)} %slice_bitcast_fusion), channel_id=1, source_target_pairs={{4,0},{8,4},{12,8},{16,12},{20,16},{24,20},{28,24},{32,28},{36,32}... | collective-permute-start | bytes 86024 | tf_op jit(solution)/shard_map/ppermute | solution.py:26
  244.8 3.8 %copy-start = (bf16[2,3,448,512]{3,2,1,0:T(8,128)(2,1)S(1)}, bf16[2,3,448,512]{3,2,1,0:T(8,128)(2,1)}, u32[]{:S(2)}) copy-start(bf16[2,3,448,512]{3,2,1,0:T(8,128)(2,1)} %get-tuple-element.11) | copy-start | bytes 8257540
  248.5 1.5 copy-start.1

commit v4 on v3

--- a/solution.py
+++ b/solution.py
@@ -54,6 +54,7 @@
         self.send, self.recv = send, recv
         self.phases = 0
         self.open = []
+        self.singles = []
 
     def copy(self, src, dst, ph, slot_s, slot_r, axis, to):
         return pltpu.make_async_remote_copy(
@@ -86,7 +87,18 @@
 
         lax.fori_loop(1, size, body, 0)
 
+    def phase(self):
+        self.phases += 1
+        return self.phases - 1
+
+    def one(self, src, dst, ph, slot_s, slot_r, axis, to):
+        copy = self.copy(src, dst, ph, slot_s, slot_r, axis, to)
+        copy.start()
+        self.singles.append(copy)
+
     def drain(self):
+        for copy in self.singles:
+            copy.wait_send()
         for ph, axis, size, me, src_of in self.open:
 
             def body(o, c):
@@ -116,7 +128,7 @@
 
 
 def chain_kernel(S, Q, X, C, D, slots, g2, w, mh, own, ahead, cot, ng, eg, hg, slr, gains, asks,
-                 ext, hsend, hrow, se, sc, pka, pkb, landa, landb, meta, mland, rows, ret, rb, xr, do, gu, lg, da,
+                 ext, hsend, hrow, se, sc, pka, pkb, landa, landb, meta, mland, rows, ret, rb, xr, do, gu, lg, ly, cmb, gf, da,
                  ld, act, dg, op, lo, pv, ss, ssl, od, gsv, hid, hgs, es, mx, dmx, ad, sls, gacc, gsrc, gland,
                  gown, gland2, send, recv, xsend, xrecv):
     me = lax.axis_index("seq")
@@ -243,18 +255,39 @@
     def gather_dp_wait(ph, k, dst):
         dp_wait(ph, lambda frm: dst.at[k, rowslice(frm), :])
 
-    def gate_up(k):
+    def gate_up(k, work=None):
+        far = [h for h in reversed(near)] + [0]
         for half in range(2):
-            full = dot_nn(xr[k], w[k, half]).astype(BF16)
+            full = dot_nn(xr[k], w[k, half])
             for q in range(CG):
-                gu[k, q, half] = full[:, q * PC:(q + 1) * PC]
-        ph = seq_start(piece_of(gu.at[k]), lg.at[k, me])
-        lg[k, me] = gu[k, cg, :, rowslice(rg), :]
-        return ph
-
-    def gate_up_wait(ph, k):
-        seq_wait(ph, lambda frm: lg.at[k, frm])
-        return add_up(lg.at[k])
+                cols = slice(q * PC, (q + 1) * PC)
+                gf[q, half] = full[:, cols]
+                gu[k, q, half] = full[:, cols].astype(BF16)
+
+        def piece(ref, t):
+            return ref.at[lax.rem(t, CG), :, rowslice(t // CG), :]
+
+        ph = wires.phase()
+        for h in far:
+            z = lax.rem(zme + h, n)
+            wires.one(piece(gu.at[k], at_z(h, 1 - yme)), ly.at[k, z], ph, h, h, "seq", yn)
+        ph2 = wires.phase()
+        for h in far:
+            z = lax.rem(zme + h, n)
+            wires.copy(ly.at[k, z], ly.at[k, z], ph, h, h, "seq", yn).wait_recv()
+            both = piece(gf, at_z(h, yme))[...] + ly[k, z].astype(F32)
+            if h == 0:
+                total = both
+            else:
+                cmb[k, z] = both.astype(BF16)
+                wires.one(cmb.at[k, z], lg.at[k, zme], ph2, h, h, "seq", at_z(h, yme))
+        if work is not None:
+            work()
+        for h in near:
+            z = lax.rem(zme + n - h, n)
+            wires.copy(lg.at[k, z], lg.at[k, z], ph2, h, h, "seq", at_z(n - h, yme)).wait_recv()
+            total = total + lg[k, z].astype(F32)
+        return total
 
     def add_up(ref):
         total = ref[0].astype(F32)
@@ -277,6 +310,33 @@
     def spread_piece(ref):
         mine = ref.at[cg, :, rowslice(rg), :]
         return seq_start(lambda to: mine, mine)
+
+    n = S // 2
+    zme, yme = me // 2, lax.rem(me, 2)
+    yn = me + 1 - 2 * yme
+    near = sorted(range(1, n), key=lambda h: (min(h, n - h), h))
+
+    def at_z(h, parity):
+        return 2 * lax.rem(zme + h, n) + parity
+
+    def spread(ref, work=None):
+        def piece(t):
+            return ref.at[lax.rem(t, CG), :, rowslice(t // CG), :]
+
+        ph = wires.phase()
+        mine = piece(me)
+        for h in reversed(near):
+            wires.one(mine, mine, ph, h, h, "seq", at_z(h, yme))
+        wires.one(mine, mine, ph, 0, n, "seq", yn)
+        for h in near:
+            frm = at_z(n - h, yme)
+            wires.copy(piece(frm), piece(frm), ph, h, h, "seq", frm).wait_recv()
+            wires.one(piece(frm), piece(frm), ph, n + h, n + h, "seq", yn)
+        if work is not None:
+            work()
+        for h in [0] + near:
+            frm = at_z(n - h, 1 - yme)
+            wires.copy(piece(frm), piece(frm), ph, n + h, n + h, "seq", yn).wait_recv()
 
     def spread_wait(ph, ref):
         seq_wait(ph, lambda frm: ref.at[lax.rem(frm, CG), :, rowslice(frm // CG), :])
@@ -511,18 +571,15 @@
     seq_wait(ph_e, lambda frm: landa.at[1, frm])
     unpack(2, landa.at[1], PK, 0)
     gather_dp_wait(ph_x, 0, xr)
-    ph = gate_up(0)
-    gsv[0] = gate_up_wait(ph, 0)
+    gsv[0] = gate_up(0)
     act_piece(0)
-    ph = spread_piece(act.at[0])
-    bulk(0, 3 * NC // 8)
-    spread_wait(ph, act.at[0])
+    spread(act.at[0])
     out = None
     for q in range(CG):
         part = dot_nt(act[0, q, 0], w[0, 2, :, q * PC:(q + 1) * PC])
         out = part if out is None else out + part
     ph = reduce_dp(0, out)
-    bulk(3 * NC // 8, NC // 2)
+    bulk(0, NC // 8)
     seq_wait(ph_m, lambda frm: mland.at[frm])
     facts = jnp.sum(mland[...], axis=1)
 
@@ -548,6 +605,7 @@
         pv[(C + j) * S:(C + j + 1) * S, :] = before
         cols.append(jnp.sum(before * before, axis=1, keepdims=True))
     ph = sums_start(0, cols)
+    bulk(NC // 8, 2 * NC // 8)
     gain_h, gain_e = g2[0:1, :], g2[1:2, :]
     scale = lax.rsqrt(sums_wait(ph, 0) + eps_norm)
 
@@ -558,18 +616,17 @@
     xr[1, rowslice(d), :] = od[3 * RW:4 * RW, :]
     ph = gather_dp(1, xr)
     ph_r0 = send_back(0)
+    bulk(2 * NC // 8, 3 * NC // 8)
     gather_dp_wait(ph, 1, xr)
-    ph = gate_up(1)
-    bulk(NC // 2, NC)
+    gsv[1] = gate_up(1, lambda: bulk(3 * NC // 8, NC // 2))
     d_act = dact_wait(ph_da2, 1)
-    gsv[1] = gate_up_wait(ph, 1)
     pre_grads(1, d_act)
-    ph = spread_piece(dg.at[1])
     act_piece(1)
+    spread(dg.at[1])
+    ph = reduce_dp(1, drows(1))
     ph_a2 = spread_piece(act.at[1])
-    spread_wait(ph, dg.at[1])
-    ph = reduce_dp(1, drows(1))
     in_grads(1)
+    bulk(NC // 2, 5 * NC // 8)
     back = reduce_dp_wait(ph, 1)
     od[RW:2 * RW, :] = back.astype(BF16)
     cols, keep_u, keep_n = [], [], []
@@ -584,6 +641,7 @@
         cols.append(jnp.sum(u * unit, axis=1, keepdims=True))
     ph = sums_start(1, cols)
 
+    bulk(5 * NC // 8, 6 * NC // 8)
     inner = sums_wait(ph, 1)
 
     for i in range(C):
@@ -592,9 +650,10 @@
     do[0, rowslice(d), :] = od[3 * RW:4 * RW, :]
     ph = gather_dp(0, do)
     ph_r1 = send_back(1)
+    bulk(6 * NC // 8, 7 * NC // 8)
     gather_dp_wait(ph, 0, do)
     ph = dact(0)
-    spread_wait(ph_a2, act.at[1])
+    bulk(7 * NC // 8, NC)
     seq_wait(ph_r0, lambda frm: ret.at[0, frm])
     seq_wait(ph_r1, lambda frm: ret.at[1, frm])
     widen(0, prev_sel, 0, prev_w)
@@ -611,15 +670,15 @@
     sweep(early, 0)
     d_act = dact_wait(ph, 0)
     pre_grads(0, d_act)
-    ph = spread_piece(dg.at[0])
-    down_grad(1)
-    down_grad(0)
-    spread_wait(ph, dg.at[0])
+    spread(dg.at[0])
     for b in range(S):
         gsrc[b] = jnp.sum(gacc[:, :, dslice(b)], axis=1)
     ph_g = seq_start(lambda to: gsrc.at[to], gland.at[me])
     gland[me] = gsrc[me]
     ph = reduce_dp(2, drows(0))
+    spread_wait(ph_a2, act.at[1])
+    down_grad(1)
+    down_grad(0)
     in_grads(0)
     back = reduce_dp_wait(ph, 2)
     od[2 * RW:3 * RW, :] = back.astype(BF16)
@@ -679,7 +738,7 @@
     PC = HS // CG
     NC = T // PK
     vm = pltpu.VMEM
-    phases = 30
+    phases = 32
     return pl.pallas_call(
         functools.partial(chain_kernel, S, Q, X, C, D),
         out_shape=(
@@ -709,7 +768,10 @@
             vm((2, NR, DS), BF16),
             vm((2, NR, DS), BF16),
             vm((2, CG, 2, NR, PC), BF16),
-            vm((2, S, 2, RW, PC), BF16),
+            vm((2, S // 2, 2, RW, PC), BF16),
+            vm((2, S // 2, 2, RW, PC), BF16),
+            vm((2, S // 2, 2, RW, PC), BF16),
+            vm((CG, 2, NR, PC), F32),
             vm((2, CG, 1, NR, PC), BF16),
             vm((2, S, 1, RW, PC), BF16),
             vm((2, CG, 1, NR, PC), BF16),

time: 251 us -> 235 us (0.936)
  Pallas kernels: 232 us -> 216 us
    pallas_call x1, Pallas kernels: 232 us -> 216 us  [chain(): pl.pallas_call(functools.partial(chain_kernel, S, Q, X, C, D), out_shape=...]
where the time goes in v4:
time: 235 us
  Pallas kernels  216 us (92%)
  local copies, waits for them, and re-layouts  9.29 us (4%)
  matrix products  3.75 us (2%)
  other arithmetic  3.37 us (1%)
    pallas_call x1, Pallas kernels, chain(): pl.pallas_call(functools.partial(chain_kernel, S, Q, X, C, D), out_shape=...  216 us
  transfers between devices with their start and end apart: 1, of which 0 were waited for; matrix products, arithmetic and copies ran while one was open for 3% of the time, Pallas kernels for 0%

profile of v4, /device:TPU:1, one launch (start us, length us, event | category | flops | bytes accessed | tf_op | source)
XLA Modules:
  0.0 234.9 jit_solution(15392477538431012178)
XLA Ops:
  0.6 0.9 slice_bitcast_fusion
  1.6 1.3 collective-permute-start
  2.9 0.8 reshape_squeeze.3
  3.6 0.8 fusion.10
  4.4 0.8 squeeze.12
  5.1 0.8 bitcast_select_fusion
  5.9 0.7 fusion.11
  6.7 0.1 lt.27
  6.8 0.2 select_multiply_fusion
  7.0 0.1 mul.48
  7.1 0.1 reshape.71
  7.2 0.8 slice.48
  8.0 0.1 dynamic-slice_bitcast_fusion
  8.1 0.1 fusion.8
  8.1 1.6 reshape.72.ng
  9.8 0.6 concatenate.7.g2
  10.4 0.6 stack.44.slots
  11.0 0.0 collective-permute-done
  11.0 0.7 pad.42.ahead
  11.7 216.4 %expert_chain.1 = (bf16[2,3,448,512]{3,2,1,0:T(8,128)(2,1)}, bf16[128,7168]{1,0:T(8,128)(2,1)}, bf16[16,7168]{1,0:T(8,128)(2,1)}, f32[4,112]{1,0:T(4,128)}, f32[8,128]{1,0:T(8,128)}) custom-call(f32[8,128]{1,0:T(8,128)} %stack.44.slots, f32[8,448]{1,0:T(8,128)} %concatenate.7.g2, bf16[2,3,448,512]{3,2,1,0:T(8,128)(2,1)} %w.1, bf16[128,7168]{1,0:T(8,128)(2,1)} %bitcast.49, ...), custom_call_target="tpu_custom_call" | custom-call | tf_op jit(solution)/shard_map/expert_chain/pallas_call | solution.py:742
  228.2 0.7 fusion.7
  228.9 0.1 convert_reduce_fusion
  229.0 0.0 copy-start
  229.0 3.7 %fusion.1 = bf16[1,1,128,7168]{3,2,1,0:T(8,128)(2,1)} fusion(bf16[128,7168]{1,0:T(8,128)(2,1)} %get-tuple-element.10, pred[128]{0:T(512)(128)(4,1)S(1)} %broadcast_compare_fusion, bf16[16,7168]{1,0:T(8,128)(2,1)} %get-tuple-element.9, s32[12]{0:T(128)S(1)} %fusion.7), kind=kOutput, calls=%fused_computation.2 | convolution fusion | flops 23856640 | bytes 3899568 | tf_op jit(solution)/shard_map/dot_general | solution.py:852
  232.8 0.0 copy-done
  232.8 0.0 copy-start.1
  232.8 1.5 copy.13
  234.3 0.0 copy-done.1
  234.3 0.6 copy.14
  (12 shorter events, 0.1 us)
Async XLA Ops:
  1.6 9.5 %collective-permute-start = (bf16[2,7168]{1,0:T(2,128)(2,1)S(1)}, bf16[2,7168]{1,0:T(2,128)(2,1)S(1)}, u32[]{:S(2)}, u32[]{:S(2)}) collective-permute-start(bf16[2,7168]{1,0:T(2,128)(2,1)S(1)} %slice_bitcast_fusion), channel_id=1, source_target_pairs={{4,0},{8,4},{12,8},{16,12},{20,16},{24,20},{28,24},{32,28},{36,32}... | collective-permute-start | bytes 86024 | tf_op jit(solution)/shard_map/ppermute | solution.py:26
  229.0 3.8 %copy-start = (bf16[2,3,448,512]{3,2,1,0:T(8,128)(2,1)S(1)}, bf16[2,3,448,512]{3,2,1,0:T(8,128)(2,1)}, u32[]{:S(2)}) copy-start(bf16[2,3,448,512]{3,2,1,0:T(8,128)(2,1)} %get-tuple-element.11) | copy-start | bytes 8257540
  232.8 1.5 copy-start.1

commit v5 on v4

--- a/solution.py
+++ b/solution.py
@@ -127,9 +127,9 @@
     return lambda: pl.semaphore_wait(barrier, total)
 
 
-def chain_kernel(S, Q, X, C, D, slots, g2, w, mh, own, ahead, cot, ng, eg, hg, slr, gains, asks,
+def chain_kernel(S, Q, X, C, D, slots, w, mh, own, ahead, cot, ng, eg, hg, slr, gains, asks,
                  ext, hsend, hrow, se, sc, pka, pkb, landa, landb, meta, mland, rows, ret, rb, xr, do, gu, lg, ly, cmb, gf, da,
-                 ld, act, dg, op, lo, pv, ss, ssl, od, gsv, hid, hgs, es, mx, dmx, ad, sls, gacc, gsrc, gland,
+                 ld, act, dg, op, lo, pv, ss, ssl, od, gsv, hid, hgs, es, mx, dmx, dmu, ad, sls, gacc, gsrc, gland,
                  gown, gland2, send, recv, xsend, xrecv):
     me = lax.axis_index("seq")
     d = lax.axis_index("dp")
@@ -206,7 +206,8 @@
     slot_tok, slot_live, slot_w = column(slot_row), column(live_row), column(weight_row)
 
     ext[0:T, :] = own[...]
-    ext[T:T + PK, :] = ahead[...]
+    ext[T:T + PK, :] = jnp.zeros((PK, D), BF16)
+    ext[T:T + 2, :] = ahead[...]
     wide = lax.broadcasted_iota(jnp.int32, (PK, T + PK), 1).astype(F32)
     for k in range(2):
         se[k] = dot_nn(jnp.where(wide == slot_tok + (k + 1.0), 1.0, 0.0).astype(BF16), ext[...]).astype(BF16)
@@ -359,14 +360,23 @@
             total = part if total is None else total + part
         return total
 
-    def sums_start(n, cols):
-        lane = lax.broadcasted_iota(jnp.int32, (S, 128), 1)
-        total = jnp.zeros((S, 128), F32)
+    laneS = lax.broadcasted_iota(jnp.int32, (S, 128), 1)
+    lineS = lax.broadcasted_iota(jnp.int32, (S, 128), 0)
+
+    def to_row(cols):
+        total = jnp.zeros((1, 128), F32)
         for i, col in enumerate(cols):
-            total = total + jnp.where(lane == i, col, 0.0)
-        ss[n] = total
-        ph = seq_start(lambda to: ss.at[n], ssl.at[n, me])
-        ssl[n, me] = total
+            total = total + jnp.sum(jnp.where(laneS == lineS + i * S, col, 0.0), axis=0, keepdims=True)
+        return total
+
+    def to_col(row, i):
+        return jnp.sum(jnp.where(laneS == lineS + i * S, row, 0.0), axis=1, keepdims=True)
+
+    def sums_start(k, cols):
+        ss[k, 0:1, :] = to_row(cols[:C])
+        ss[k, 1:2, :] = to_row(cols[C:])
+        ph = seq_start(lambda to: ss.at[k], ssl.at[k, me])
+        ssl[k, me] = ss[k]
         return ph
 
     def sums_wait(ph, n):
@@ -404,7 +414,7 @@
         return [jnp.sum(t, axis=1, keepdims=True) * (1.0 / D) for t in total]
 
     def gain(k, at):
-        return ng[k:k + 1, at]
+        return ng[k // 2, k % 2:k % 2 + 1, at]
 
     def collect(k, at, value, mask):
         value = value * mask
@@ -457,13 +467,13 @@
                 collect(0, at, dm1 * n1, mask)
                 collect(1, at, dm1 * (e_at(0, at) * se1), mask)
             u = dm1 * gain(0, at)
-            dmx[:, at] = u
+            dmu[:, at] = u
             return (acc[0] + u * n1,)
 
         inner, = sweep(low, 1)
 
         def last(at, acc):
-            store(at, ((dmx[:, at] - (h_at(at) * sh) * inner) * sh).astype(BF16))
+            store(at, (dmu[:, at] - (h_at(at) * sh) * inner) * sh)
             return acc
 
         sweep(last, 0)
@@ -487,7 +497,7 @@
         sh, se1 = rows_pass_1(h_at, e_at, lambda at: cot[chunk(c), at].astype(F32), mask, None, None)
 
         def store(at, value):
-            hgs[chunk(c), at] = value
+            hgs[chunk(c), at] = value.astype(BF16)
 
         rows_pass_2(h_at, e_at, mask, sh, se1, None, store)
         hg_copy(c).start()
@@ -606,11 +616,14 @@
         cols.append(jnp.sum(before * before, axis=1, keepdims=True))
     ph = sums_start(0, cols)
     bulk(NC // 8, 2 * NC // 8)
-    gain_h, gain_e = g2[0:1, :], g2[1:2, :]
+    gain_h, gain_e = jnp.zeros((1, DS), F32), jnp.zeros((1, DS), F32)
+    for b in range(S):
+        gain_h = gain_h + jnp.where(me == b, ng[1, 0:1, dslice(b)], 0.0)
+        gain_e = gain_e + jnp.where(me == b, ng[1, 1:2, dslice(b)], 0.0)
     scale = lax.rsqrt(sums_wait(ph, 0) + eps_norm)
 
     for j in range(C):
-        unit = pv[(C + j) * S:(C + j + 1) * S, :] * scale[:, C + j:C + j + 1]
+        unit = pv[(C + j) * S:(C + j + 1) * S, :] * to_col(scale[1:2], j)
         mixed = unit * gain_h + (rows_at(2, C + j) * fact(8 + j)) * gain_e
         od[3 * RW + j * S:3 * RW + (j + 1) * S, :] = mixed.astype(BF16)
     xr[1, rowslice(d), :] = od[3 * RW:4 * RW, :]
@@ -635,7 +648,7 @@
         for j in range(C):
             top = top + ov(j, i) * back[j * S:(j + 1) * S]
         u = top * gain_h
-        unit = pv[i * S:(i + 1) * S, :] * scale[:, i:i + 1]
+        unit = pv[i * S:(i + 1) * S, :] * to_col(scale[0:1], i)
         keep_u.append(u)
         keep_n.append(unit)
         cols.append(jnp.sum(u * unit, axis=1, keepdims=True))
@@ -645,7 +658,7 @@
     inner = sums_wait(ph, 1)
 
     for i in range(C):
-        back = (keep_u[i] - keep_n[i] * inner[:, i:i + 1]) * scale[:, i:i + 1]
+        back = (keep_u[i] - keep_n[i] * to_col(inner[0:1], i)) * to_col(scale[0:1], i)
         od[3 * RW + i * S:3 * RW + (i + 1) * S, :] = (back * fact(i)).astype(BF16)
     do[0, rowslice(d), :] = od[3 * RW:4 * RW, :]
     ph = gather_dp(0, do)
@@ -668,6 +681,12 @@
         return acc
 
     sweep(early, 0)
+
+    def early_store(at, value):
+        sls[1, :, at] = value[8:].astype(BF16)
+
+    back_early = hop(sls.at[1], slr.at[1], 2 * NC + 3, before_me)
+    back_rows = hop(sls.at[0], slr.at[0], 2 * NC, before_me)
     d_act = dact_wait(ph, 0)
     pre_grads(0, d_act)
     spread(dg.at[0])
@@ -676,6 +695,8 @@
     ph_g = seq_start(lambda to: gsrc.at[to], gland.at[me])
     gland[me] = gsrc[me]
     ph = reduce_dp(2, drows(0))
+    rows_pass_2(slot_h, slot_e, None, slot_sh, slot_se1, None, early_store)
+    back_early.start()
     spread_wait(ph_a2, act.at[1])
     down_grad(1)
     down_grad(0)
@@ -708,10 +729,9 @@
     widen(2, prev_sel, 2, None)
 
     def slot_store(at, value):
-        sls[:, at] = value
+        sls[0, :, at] = value[:8].astype(BF16)
 
     rows_pass_2(slot_h, slot_e, None, slot_sh, slot_se1, lambda at: ad[2, :, at], slot_store)
-    back_rows = hop(sls, slr, 2 * NC, before_me)
     back_rows.start()
     dp_wait(ph_q, lambda frm: gland2.at[frm])
     gains[...] = add_up(gland2)
@@ -725,10 +745,11 @@
     ask_hop.wait_send()
     row_hop.wait_send()
     back_rows.wait()
+    back_early.wait()
     wires.drain()
 
 
-def chain(slots, g2, w, mh, own, ahead, cot, ng, C):
+def chain(slots, w, mh, own, ahead, cot, ng, C):
     S, Q, X = lax.axis_size("seq"), lax.axis_size("dp"), lax.axis_size("section")
     DS, HS = w.shape[2], w.shape[3]
     T, D = mh.shape
@@ -744,11 +765,11 @@
         out_shape=(
             jax.ShapeDtypeStruct(w.shape, BF16),
             jax.ShapeDtypeStruct((T, D), BF16),
-            jax.ShapeDtypeStruct((PK, D), BF16),
+            jax.ShapeDtypeStruct((2, 8, D), BF16),
             jax.ShapeDtypeStruct((4, DS // Q), F32),
             jax.ShapeDtypeStruct((8, 128), F32),
         ),
-        in_specs=[pl.BlockSpec(memory_space=vm)] * 8,
+        in_specs=[pl.BlockSpec(memory_space=vm)] * 7,
         out_specs=(pl.BlockSpec(memory_space=vm),) * 5,
         scratch_shapes=[
             vm((T + PK, D), BF16),
@@ -779,8 +800,8 @@
             vm((3, NR, DS), BF16),
             vm((3, Q, RW, DS), BF16),
             vm((2 * RW, DS), F32),
-            vm((2, S, 128), F32),
-            vm((2, S, S, 128), F32),
+            vm((2, 2, 128), F32),
+            vm((2, S, 2, 128), F32),
             vm((4 * RW, DS), BF16),
             vm((2, 2, RW, PC), F32),
             vm((T, D), BF16),
@@ -788,8 +809,9 @@
             vm((2 * PK, D), BF16),
             vm((PK, D), F32),
             vm((PK, D), F32),
+            vm((PK, D), F32),
             vm((3, PK, D), F32),
-            vm((PK, D), BF16),
+            vm((2, 8, D), BF16),
             vm((4, 8, D), F32),
             vm((S, 4, DS), F32),
             vm((S, 4, DS), F32),
@@ -797,14 +819,14 @@
             vm((Q, 4, DS // Q), F32),
             pltpu.SemaphoreType.DMA((phases, S)),
             pltpu.SemaphoreType.DMA((phases, S)),
-            pltpu.SemaphoreType.DMA((2 * NC + 3,)),
-            pltpu.SemaphoreType.DMA((2 * NC + 3,)),
+            pltpu.SemaphoreType.DMA((2 * NC + 4,)),
+            pltpu.SemaphoreType.DMA((2 * NC + 4,)),
         ],
         compiler_params=pltpu.CompilerParams(
             collective_id=0, has_side_effects=True, vmem_limit_bytes=60 * 1024 * 1024
         ),
         name="expert_chain",
-    )(slots, g2, w, mh, own, ahead, cot, ng)
+    )(slots, w, mh, own, ahead, cot, ng)
 
 
 def pick(index, count):
@@ -840,17 +862,13 @@
         lanes(live[1]),
         lanes(flat[:1].astype(F32) * 0.0),
     ])
-    g2 = lax.dynamic_slice(norm_gain[1], (0, me * DS), (2, DS))
-    g2 = jnp.concatenate([g2, jnp.zeros((6, DS), F32)], 0)
-    ahead = jnp.pad(ahead, ((0, PK - 2), (0, 0)))
-    ng = norm_gain.reshape(4, D)
-
-    expert_grad, grads, slot_grads, total, asks = chain(slots, g2, w, mh, own, ahead, cot, ng, C)
+
+    expert_grad, grads, slot_grads, total, asks = chain(slots, w, mh, own, ahead, cot, norm_gain, C)
     back_to = jnp.where(asks[3, :2 * C] > 0.5, asks[0, :2 * C], -1.0).astype(jnp.int32)
     put = pick(back_to, tokens_here)
     hit = jnp.sum(put.astype(F32), axis=0)
     placed = lax.dot_general(
-        put, slot_grads[:2 * C], (((0,), (0,)), ((), ())), preferred_element_type=F32
+        put, slot_grads.reshape(PK, D)[:2 * C], (((0,), (0,)), ((), ())), preferred_element_type=F32
     )
     hidden_grad = jnp.where(hit[:, None] > 0.5, placed.astype(BF16), grads)
     return (hidden_grad[None, None], expert_grad[None], total.reshape(1, 2, 2, -1))

time: 235 us -> 228 us (0.970)
  local copies, waits for them, and re-layouts: 9.29 us -> 6.05 us
  Pallas kernels: 216 us -> 213 us
    pallas_call x1, Pallas kernels: 216 us -> 213 us  [chain(): pl.pallas_call(functools.partial(chain_kernel, S, Q, X, C, D), out_shape=...]
  transfers between devices with their start and end apart: 1 -> 1, of which waited for: 0 -> 0; matrix products, arithmetic and copies ran while one was open for 3% -> 2% of each run, Pallas kernels for 0% -> 0%
where the time goes in v5:
time: 228 us
  Pallas kernels  213 us (93%)
  local copies, waits for them, and re-layouts  6.05 us (3%)
  matrix products  3.75 us (2%)
  other arithmetic  3.39 us (1%)
    pallas_call x1, Pallas kernels, chain(): pl.pallas_call(functools.partial(chain_kernel, S, Q, X, C, D), out_shape=...  213 us
  transfers between devices with their start and end apart: 1, of which 0 were waited for; matrix products, arithmetic and copies ran while one was open for 2% of the time, Pallas kernels for 0%

profile of v5, /device:TPU:1, one launch (start us, length us, event | category | flops | bytes accessed | tf_op | source)
XLA Modules:
  0.0 227.9 jit_solution(7005666047244049664)
XLA Ops:
  0.6 0.9 slice_bitcast_fusion
  1.6 1.3 collective-permute-start
  2.9 0.8 reshape_squeeze.3
  3.6 0.8 fusion.10
  4.4 0.8 squeeze.24
  5.1 0.8 bitcast_select_fusion
  5.9 0.7 fusion.11
  6.7 0.1 lt.24
  6.8 0.2 select_multiply_fusion
  7.0 0.1 mul.45
  7.1 0.1 reshape.70
  7.2 0.1 fusion.8
  7.2 0.6 stack.44.slots
  7.9 0.0 collective-permute-done.ahead
  7.9 0.0 copy-start.1
  7.9 0.6 copy-done.1
  8.5 212.7 %expert_chain.1 = (bf16[2,3,448,512]{3,2,1,0:T(8,128)(2,1)}, bf16[128,7168]{1,0:T(8,128)(2,1)}, bf16[2,8,7168]{2,1,0:T(8,128)(2,1)}, f32[4,112]{1,0:T(4,128)}, f32[8,128]{1,0:T(8,128)}) custom-call(f32[8,128]{1,0:T(8,128)} %stack.44.slots, bf16[2,3,448,512]{3,2,1,0:T(8,128)(2,1)} %w.1, bf16[128,7168]{1,0:T(8,128)(2,1)} %bitcast.48, ...), custom_call_target="tpu_custom_call" | custom-call | tf_op jit(solution)/shard_map/expert_chain/pallas_call | solution.py:763
  221.1 0.8 fusion.7
  221.9 0.1 convert_reduce_fusion
  222.0 0.0 copy-start
  222.0 3.7 %fusion.1 = bf16[1,1,128,7168]{3,2,1,0:T(8,128)(2,1)} fusion(bf16[128,7168]{1,0:T(8,128)(2,1)} %get-tuple-element.10, pred[128]{0:T(512)(128)(4,1)S(1)} %broadcast_compare_fusion, bf16[16,7168]{1,0:T(8,128)(2,1)} %bitcast.50, s32[12]{0:T(128)S(1)} %fusion.7), kind=kOutput, calls=%fused_computation.2 | convolution fusion | flops 23856640 | bytes 3899568 | tf_op jit(solution)/shard_map/dot_general | solution.py:870
  225.8 0.0 copy-done
  225.8 0.0 copy-start.2
  225.8 1.5 copy.13
  227.3 0.0 copy-done.2
  227.3 0.6 copy.14
  (12 shorter events, 0.1 us)
Async XLA Ops:
  1.6 6.3 %collective-permute-start = (bf16[2,7168]{1,0:T(2,128)(2,1)S(1)}, bf16[2,7168]{1,0:T(2,128)(2,1)S(1)}, u32[]{:S(2)}, u32[]{:S(2)}) collective-permute-start(bf16[2,7168]{1,0:T(2,128)(2,1)S(1)} %slice_bitcast_fusion), channel_id=1, source_target_pairs={{4,0},{8,4},{12,8},{16,12},{20,16},{24,20},{28,24},{32,28},{36,32}... | collective-permute-start | bytes 86024 | tf_op jit(solution)/shard_map/ppermute | solution.py:26
  7.9 0.6 copy-start.1
  222.0 3.8 %copy-start = (bf16[2,3,448,512]{3,2,1,0:T(8,128)(2,1)S(1)}, bf16[2,3,448,512]{3,2,1,0:T(8,128)(2,1)}, u32[]{:S(2)}) copy-start(bf16[2,3,448,512]{3,2,1,0:T(8,128)(2,1)} %get-tuple-element.11) | copy-start | bytes 8257540
  225.8 1.5 copy-start.2

commit v6 on v5

--- a/solution.py
+++ b/solution.py
@@ -581,15 +581,15 @@
     seq_wait(ph_e, lambda frm: landa.at[1, frm])
     unpack(2, landa.at[1], PK, 0)
     gather_dp_wait(ph_x, 0, xr)
-    gsv[0] = gate_up(0)
+    gsv[0] = gate_up(0, lambda: bulk(0, NC // 8))
     act_piece(0)
-    spread(act.at[0])
+    spread(act.at[0], lambda: bulk(NC // 8, 2 * NC // 8))
     out = None
     for q in range(CG):
         part = dot_nt(act[0, q, 0], w[0, 2, :, q * PC:(q + 1) * PC])
         out = part if out is None else out + part
     ph = reduce_dp(0, out)
-    bulk(0, NC // 8)
+    bulk(2 * NC // 8, 3 * NC // 8)
     seq_wait(ph_m, lambda frm: mland.at[frm])
     facts = jnp.sum(mland[...], axis=1)
 
@@ -615,7 +615,7 @@
         pv[(C + j) * S:(C + j + 1) * S, :] = before
         cols.append(jnp.sum(before * before, axis=1, keepdims=True))
     ph = sums_start(0, cols)
-    bulk(NC // 8, 2 * NC // 8)
+    bulk(3 * NC // 8, 4 * NC // 8)
     gain_h, gain_e = jnp.zeros((1, DS), F32), jnp.zeros((1, DS), F32)
     for b in range(S):
         gain_h = gain_h + jnp.where(me == b, ng[1, 0:1, dslice(b)], 0.0)
@@ -629,9 +629,8 @@
     xr[1, rowslice(d), :] = od[3 * RW:4 * RW, :]
     ph = gather_dp(1, xr)
     ph_r0 = send_back(0)
-    bulk(2 * NC // 8, 3 * NC // 8)
     gather_dp_wait(ph, 1, xr)
-    gsv[1] = gate_up(1, lambda: bulk(3 * NC // 8, NC // 2))
+    gsv[1] = gate_up(1, lambda: bulk(4 * NC // 8, 5 * NC // 8))
     d_act = dact_wait(ph_da2, 1)
     pre_grads(1, d_act)
     act_piece(1)
@@ -639,7 +638,7 @@
     ph = reduce_dp(1, drows(1))
     ph_a2 = spread_piece(act.at[1])
     in_grads(1)
-    bulk(NC // 2, 5 * NC // 8)
+    bulk(5 * NC // 8, 6 * NC // 8)
     back = reduce_dp_wait(ph, 1)
     od[RW:2 * RW, :] = back.astype(BF16)
     cols, keep_u, keep_n = [], [], []
@@ -654,7 +653,7 @@
         cols.append(jnp.sum(u * unit, axis=1, keepdims=True))
     ph = sums_start(1, cols)
 
-    bulk(5 * NC // 8, 6 * NC // 8)
+    bulk(6 * NC // 8, 7 * NC // 8)
     inner = sums_wait(ph, 1)
 
     for i in range(C):
@@ -663,10 +662,9 @@
     do[0, rowslice(d), :] = od[3 * RW:4 * RW, :]
     ph = gather_dp(0, do)
     ph_r1 = send_back(1)
-    bulk(6 * NC // 8, 7 * NC // 8)
+    bulk(7 * NC // 8, NC)
     gather_dp_wait(ph, 0, do)
     ph = dact(0)
-    bulk(7 * NC // 8, NC)
     seq_wait(ph_r0, lambda frm: ret.at[0, frm])
     seq_wait(ph_r1, lambda frm: ret.at[1, frm])
     widen(0, prev_sel, 0, prev_w)

time: 228 us -> 228 us (level)
  no operation moved by 1% of the time
where the time goes in v6:
time: 228 us; the launch traced here: 227 us
  Pallas kernels  212 us (93%)
  local copies, waits for them, and re-layouts  6.05 us (3%)
  matrix products  3.75 us (2%)
  other arithmetic  3.39 us (1%)
    pallas_call x1, Pallas kernels, chain(): pl.pallas_call(functools.partial(chain_kernel, S, Q, X, C, D), out_shape=...  212 us
  transfers between devices with their start and end apart: 1, of which 0 were waited for; matrix products, arithmetic and copies ran while one was open for 2% of the time, Pallas kernels for 0%

profile of v6, /device:TPU:1, one launch (start us, length us, event | category | flops | bytes accessed | tf_op | source)
XLA Modules:
  0.0 227.3 jit_solution(301848201506314323)
XLA Ops:
  0.6 0.9 slice_bitcast_fusion
  1.6 1.3 collective-permute-start
  2.9 0.8 reshape_squeeze.3
  3.6 0.8 fusion.10
  4.4 0.8 squeeze.24
  5.1 0.8 bitcast_select_fusion
  5.9 0.7 fusion.11
  6.7 0.1 lt.24
  6.8 0.2 select_multiply_fusion
  7.0 0.1 mul.45
  7.1 0.1 reshape.70
  7.2 0.1 fusion.8
  7.2 0.6 stack.44.slots
  7.9 0.0 collective-permute-done.ahead
  7.9 0.0 copy-start.1
  7.9 0.6 copy-done.1
  8.5 212.1 %expert_chain.1 = (bf16[2,3,448,512]{3,2,1,0:T(8,128)(2,1)}, bf16[128,7168]{1,0:T(8,128)(2,1)}, bf16[2,8,7168]{2,1,0:T(8,128)(2,1)}, f32[4,112]{1,0:T(4,128)}, f32[8,128]{1,0:T(8,128)}) custom-call(f32[8,128]{1,0:T(8,128)} %stack.44.slots, bf16[2,3,448,512]{3,2,1,0:T(8,128)(2,1)} %w.1, bf16[128,7168]{1,0:T(8,128)(2,1)} %bitcast.48, ...), custom_call_target="tpu_custom_call" | custom-call | tf_op jit(solution)/shard_map/expert_chain/pallas_call | solution.py:761
  220.6 0.8 fusion.7
  221.4 0.1 convert_reduce_fusion
  221.5 0.0 copy-start
  221.5 3.7 %fusion.1 = bf16[1,1,128,7168]{3,2,1,0:T(8,128)(2,1)} fusion(bf16[128,7168]{1,0:T(8,128)(2,1)} %get-tuple-element.10, pred[128]{0:T(512)(128)(4,1)S(1)} %broadcast_compare_fusion, bf16[16,7168]{1,0:T(8,128)(2,1)} %bitcast.50, s32[12]{0:T(128)S(1)} %fusion.7), kind=kOutput, calls=%fused_computation.2 | convolution fusion | flops 23856640 | bytes 3899568 | tf_op jit(solution)/shard_map/dot_general | solution.py:868
  225.2 0.0 copy-done
  225.2 0.0 copy-start.2
  225.2 1.5 copy.13
  226.8 0.0 copy-done.2
  226.8 0.6 copy.14
  (12 shorter events, 0.1 us)
Async XLA Ops:
  1.6 6.3 %collective-permute-start = (bf16[2,7168]{1,0:T(2,128)(2,1)S(1)}, bf16[2,7168]{1,0:T(2,128)(2,1)S(1)}, u32[]{:S(2)}, u32[]{:S(2)}) collective-permute-start(bf16[2,7168]{1,0:T(2,128)(2,1)S(1)} %slice_bitcast_fusion), channel_id=1, source_target_pairs={{4,0},{8,4},{12,8},{16,12},{20,16},{24,20},{28,24},{32,28},{36,32}... | collective-permute-start | bytes 86024 | tf_op jit(solution)/shard_map/ppermute | solution.py:26
  7.9 0.6 copy-start.1
  221.5 3.8 %copy-start = (bf16[2,3,448,512]{3,2,1,0:T(8,128)(2,1)S(1)}, bf16[2,3,448,512]{3,2,1,0:T(8,128)(2,1)}, u32[]{:S(2)}) copy-start(bf16[2,3,448,512]{3,2,1,0:T(8,128)(2,1)} %get-tuple-element.11) | copy-start | bytes 8257540
  225.2 1.5 copy-start.2
